TPU v7x, 256 devices: a whole 4x4x8 slice. The times are simulated.
256 devices in a mesh: group: 8 (over y, core), leaf: 32 (over z, x).
Axes of the slice: x: 4, y: 4, z: 8, core: 2. Of those that a mesh axis runs over, the one named last changes fastest.
Arguments:
- points: float32 [3, 524288], P(None, ('group', 'leaf')), may hold values from 0 to 1
- rhs: float32 [16, 524288], P(None, ('group', 'leaf')), may hold values from -0.5 to 0.5
- counts: int32 [4096], P(('group', 'leaf')), may hold values from 32 to 128
- basis: float32 [4096, 128, 32], P(('group', 'leaf')), may hold values from -1 to 1
- leaf_geom: float32 [4096, 4], P(('group', 'leaf')), may hold values from 0.05 to 1
- leaf_partners: int32 [4096, 16], P(('group', 'leaf')), may hold values from -16 to 16, as said below
- leaf_middle_owner: int32 [256, 16], P(('group', 'leaf')), may hold values from 0 to 7, never falling along the last dimension, each value on 1 to 4 neighbouring positions
- leaf_basis_transfer: float32 [4096, 32, 32], P(('group', 'leaf')), may hold values from -1 to 1
- mid_geom: float32 [2048, 4], P(('group', 'leaf')), may hold values from 0.05 to 1
- mid_parent: int32 [8, 256], P('group', 'leaf'), may hold values from 0 to 15, never falling along the last dimension, each value on 1 to 32 neighbouring positions
- mid_transfer: float32 [2048, 32, 32], P(('group', 'leaf')), may hold values from -1 to 1
- mid_peers: int32 [2048, 8], P(('group', 'leaf')), may hold values from 0 to 31, all different within a row; in each aligned block of 8 rows (0 to 7, 8 to 15, ...) at most 4 rows name the same one
- mid_slots: int32 [2048, 8], P(('group', 'leaf')), may hold values from 0 to 7
- top_geom: float32 [128, 4], P('group'), may hold values from 0.05 to 1
- top_offsets: int32 [128, 16], P('group'), may hold values from 1 to 127
Outputs:
- product: float32 [16, 524288], P(None, ('group', 'leaf'))
Inputs may be any that keep to these rules, and one draw needn't show every extreme that they name: `leaf_partners`: column 0 is 0. Every partner leaf lies in the same group, at most 16 leaves away. `mid_peers`: over the rows of one device, no device is named more than 4 times, and some device is named exactly 4 times; the names in a row differ. `leaf_middle_owner`: never falling along a row. `mid_parent`: never falling along a row.
All inputs are finite; a program needn't handle non-finite values.
Results may differ from a plain program's by a relative error of at most 0.00013.
Values sent between devices are 32-bit elements; how exact they have to be, the bound alone decides.
A program may use at most 64 MiB of HBM per device.

v0:
```python
import jax
import jax.numpy as jnp
from jax import lax
from jax.sharding import PartitionSpec as P

PTS = 128
RANK = 32
RHS = 16
TOP = 16
NEAR = 8
REACH = 16


exact_product = lax.Precision.HIGHEST
root_three = 1.7320508075688772
length_scale = 0.5


def extended(block, sides, width):
    for axis, dim in sides:
        count = lax.axis_size(axis)
        forward = [(i, i + 1) for i in range(count - 1)]
        backward = [(target, source) for source, target in forward]
        low = lax.ppermute(
            lax.slice_in_dim(block, block.shape[dim] - width, None, axis=dim), axis, forward
        )
        high = lax.ppermute(lax.slice_in_dim(block, 0, width, axis=dim), axis, backward)
        block = jnp.concatenate([low, block, high], axis=dim)
    return block


def node_table():
    indices = jnp.arange(RANK, dtype=jnp.int32)
    layers = []
    for axis_number in range(3):
        spread = (indices * (2 * axis_number + 3) % RANK).astype(jnp.float32)
        layers.append(jnp.cos(jnp.pi * (spread + 0.5) / RANK))
    return jnp.stack(layers)


def place_nodes(geometry, table):
    return geometry[..., :3, None] + geometry[..., 3:4, None] * table


def matern(left, right):
    squared = jnp.zeros((), jnp.float32)
    for axis_number in range(3):
        difference = left[..., axis_number, :, None] - right[..., axis_number, None, :]
        squared = squared + difference * difference
    distance = jnp.sqrt(squared)
    decay_rate = root_three / length_scale
    return (1.0 + decay_rate * distance) * jnp.exp(-decay_rate * distance)


def couple_rows(target_geom, source_point_rows, table):
    coeff_width = RANK * RHS
    target_nodes = place_nodes(target_geom, table)
    source_nodes = place_nodes(source_point_rows[..., coeff_width:], table)
    source_coeff = source_point_rows[..., :coeff_width].reshape(
        source_point_rows.shape[:-1] + (RANK, RHS)
    )
    coupling = matern(target_nodes[:, None], source_nodes)
    return jnp.einsum("njkm,njmr->nkr", coupling, source_coeff, precision=exact_product)


def on_device(
    points,
    rhs,
    counts,
    basis,
    leaf_geom,
    leaf_partners,
    leaf_middle_owner,
    leaf_basis_transfer,
    mid_geom,
    mid_parent,
    mid_transfer,
    mid_peers,
    mid_slots,
    top_geom,
    top_offsets,
):
    leaf_count = counts.shape[0]
    mid_count = mid_transfer.shape[0]
    coeff_width = RANK * RHS
    table = node_table()
    position = jnp.arange(PTS, dtype=jnp.int32)
    present = (position[None, :] < counts[:, None]).astype(jnp.float32)
    masked = rhs.reshape(RHS, leaf_count, PTS) * present[None]
    stacked = jnp.concatenate([masked.reshape(RHS, leaf_count * PTS), points], axis=0)
    padded = extended(stacked, (("leaf", 1),), REACH * PTS)
    grid = padded.reshape(RHS + 3, leaf_count + 2 * REACH, PTS)
    leaf_coefficient_rows = jnp.einsum("lpk,rlp->lkr", basis, masked, precision=exact_product)
    leaf_rows = jnp.concatenate(
        [leaf_coefficient_rows.reshape(leaf_count, coeff_width), leaf_geom], axis=1
    )
    leaf_padded = extended(leaf_rows, (("leaf", 0),), REACH)
    members = (
        leaf_middle_owner[0][None, :] == jnp.arange(mid_count, dtype=jnp.int32)[:, None]
    ).astype(jnp.float32)
    upward_coefficients = jnp.einsum(
        "qcz,qct->qzt", leaf_basis_transfer, leaf_coefficient_rows, precision=exact_product
    )
    coeff_mid = jnp.einsum("ml,ljr->mjr", members, upward_coefficients, precision=exact_product)
    mid_rows = jnp.concatenate([coeff_mid.reshape(mid_count, coeff_width), mid_geom], axis=1)
    top_members = (mid_parent[0][None, :] == jnp.arange(TOP, dtype=jnp.int32)[:, None]).astype(
        jnp.float32
    )
    raised = jnp.einsum("mkj,mkr->mjr", mid_transfer, coeff_mid, precision=exact_product)
    partial_top = jnp.einsum("tm,mjr->tjr", top_members, raised, precision=exact_product)
    coeff_top = lax.psum(partial_top, "leaf")
    top_rows = jnp.concatenate([coeff_top.reshape(TOP, coeff_width), top_geom], axis=1)
    top_all = lax.all_gather(top_rows, "group", axis=0, tiled=True)
    total_tops = top_all.shape[0]
    targets = lax.axis_index("group") * TOP + jnp.arange(TOP, dtype=jnp.int32)
    top_source = (targets[:, None] + top_offsets) % total_tops
    local_top = couple_rows(top_geom, top_all[top_source], table)
    mid_all = lax.all_gather(mid_rows, "leaf", axis=0, tiled=True)
    mid_source = mid_peers * mid_count + mid_slots
    source_point_rows = mid_all[mid_source]
    device_middle_index = jnp.einsum(
        "mkj,mjr->mkr", mid_transfer, local_top[mid_parent[0]], precision=exact_product
    )
    device_middle_index = device_middle_index + couple_rows(mid_geom, source_point_rows, table)
    leaf_index = jnp.arange(leaf_count, dtype=jnp.int32)
    far_ids = leaf_index[:, None] + REACH + leaf_partners[:, NEAR:]
    local_leaf = jnp.einsum(
        "ghw,gwt->ght",
        leaf_basis_transfer,
        device_middle_index[leaf_middle_owner[0]],
        precision=exact_product,
    )
    local_leaf = local_leaf + couple_rows(leaf_geom, leaf_padded[far_ids], table)
    far_product = jnp.einsum("lpk,lkr->rlp", basis, local_leaf, precision=exact_product)
    point_cloud = points.reshape(3, leaf_count, PTS)

    def near_block(block_start):
        block_leaves = block_start * 8 + jnp.arange(8, dtype=jnp.int32)
        offsets = lax.dynamic_slice_in_dim(leaf_partners[:, :NEAR], block_start * 8, 8, 0)
        partner = block_leaves[:, None] + REACH + offsets
        target_cloud = point_cloud[:, block_leaves].transpose(1, 0, 2)
        source = grid[:, partner]
        kernel = matern(target_cloud[:, None], source[RHS:].transpose(1, 2, 0, 3))
        return jnp.einsum("bjpq,rbjq->rbp", kernel, source[:RHS], precision=exact_product)

    near_blocks = lax.map(near_block, jnp.arange(leaf_count // 8, dtype=jnp.int32))
    near_product = near_blocks.transpose(1, 0, 2, 3).reshape(RHS, leaf_count, PTS)
    product = (far_product + near_product) * present[None]
    return product.reshape(RHS, leaf_count * PTS)


def solution(mesh):
    placed = (
        P(None, ("group", "leaf")),
        P(None, ("group", "leaf")),
        P(("group", "leaf")),
        P(("group", "leaf"), None, None),
        P(("group", "leaf"), None),
        P(("group", "leaf"), None),
        P(("group", "leaf"), None),
        P(("group", "leaf"), None, None),
        P(("group", "leaf"), None),
        P("group", "leaf"),
        P(("group", "leaf"), None, None),
        P(("group", "leaf"), None),
        P(("group", "leaf"), None),
        P("group", None),
        P("group", None),
    )
    return jax.shard_map(
        on_device, mesh=mesh, in_specs=placed, out_specs=P(None, ("group", "leaf")), check_vma=False
    )
```

profile of v0, /device:TPU:32, one launch (start us, length us, event | category | flops | bytes accessed | tf_op | source)
XLA Modules:
  0.0 284.0 jit_solution(18294623102038642720)
XLA Ops:
  0.0 0.8 fusion.125
  1.0 1.4 fusion.117
  2.7 0.8 copy.62
  3.4 3.4 %collective-permute-start = (f32[16,516]{1,0:T(8,128)S(1)}, f32[16,516]{1,0:T(8,128)}, u32[]{:S(2)}, u32[]{:S(2)}) collective-permute-start(f32[16,516]{1,0:T(8,128)S(1)} %pad_maximum_fusion.4), channel_id=1, source_target_pairs={{0,1},{1,2},{2,3},{3,4},{4,5},{5,6},{6,7},{7,8},{8,9},{9,10},{10,1... | collective-permute-start | bytes 99080 | tf_op jit(solution)/shard_map/ppermute | solution.py:24
  6.8 4.6 %collective-permute-start.1 = (f32[16,516]{1,0:T(8,128)S(1)}, f32[16,516]{1,0:T(8,128)}, u32[]{:S(2)}, u32[]{:S(2)}) collective-permute-start(f32[16,516]{1,0:T(8,128)S(1)} %pad_maximum_fusion.4), channel_id=1, source_target_pairs={{1,0},{2,1},{3,2},{4,3},{5,4},{6,5},{7,6},{8,7},{9,8},{10,9},{11,1... | collective-permute-start | bytes 99080 | tf_op jit(solution)/shard_map/ppermute | solution.py:27
  11.4 0.7 lt.115
  12.2 0.9 broadcast_multiply_fusion
  13.1 0.8 pad_maximum_fusion.1
  13.9 1.9 collective-permute-start.2
  15.8 6.0 %collective-permute-start.3 = (f32[19,2048]{1,0:T(8,128)S(1)}, f32[19,2048]{1,0:T(8,128)S(1)}, u32[]{:S(2)}, u32[]{:S(2)}) collective-permute-start(f32[19,2048]{1,0:T(8,128)S(1)} %pad_maximum_fusion.1), channel_id=1, source_target_pairs={{1,0},{2,1},{3,2},{4,3},{5,4},{6,5},{7,6},{8,7},{9,8},{10,9},{11,1... | collective-permute-start | bytes 466952 | tf_op jit(solution)/shard_map/ppermute | solution.py:27
  21.9 1.3 convolution_bitcast_fusion.2
  23.2 0.9 fusion.119
  24.2 1.3 convolution_bitcast_fusion.5
  25.5 1.0 fusion.121
  26.8 135.6 %psum.7 = f32[16,512]{1,0:T(8,128)S(1)} all-reduce(f32[16,512]{1,0:T(8,128)S(1)} %reshape.345), channel_id=1, replica_groups=mesh['group'=8,'leaf'=32] {'leaf'}, use_global_device_ids=true, to_apply=%region_0.1 | all-reduce | flops 8192 | bytes 65536 | tf_op jit(solution)/shard_map/psum | solution.py:111
  162.4 0.8 copy.52
  163.2 13.4 %all_gather.6 = f32[128,516]{1,0:T(8,128)S(1)} all-gather(f32[16,516]{1,0:T(8,128)S(1)} %pad_maximum_fusion.3), channel_id=1, replica_groups=mesh['group'=8,'leaf'=32] {'group'}, dimensions={0}, use_global_device_ids=true | all-gather | bytes 297216 | tf_op jit(solution)/shard_map/all_gather | solution.py:113
  176.8 1.1 gather_fusion.2
  178.3 54.6 %all_gather.7 = f32[256,516]{1,0:T(8,128)S(1)} all-gather(f32[8,516]{1,0:T(8,128)S(1)} %pad_maximum_fusion.5), channel_id=1, replica_groups=mesh['group'=8,'leaf'=32] {'leaf'}, dimensions={0}, use_global_device_ids=true | all-gather | bytes 544896 | tf_op jit(solution)/shard_map/all_gather | solution.py:118
  233.1 0.7 gather_fusion.4
  235.2 2.7 reshape.346
  239.6 11.0 %fusion.74 = f32[16,32,16]{1,2,0:T(8,128)S(1)} fusion(f32[16,16,32,16]{3,2,1,0:T(8,128)} %reshape.346, f32[16,16,32]{2,1,0:T(8,128)S(1)} %get-tuple-element.63, f32[16,32]{1,0:T(8,128)} %get-tuple-element.72, f32[16,16,32]{2,1,0:T(8,128)S(1)} %get-tuple-element.64, f32[16,32]{1,0:T(8,128)} %get-tuple-element.73, f32[16,16,32]{2,1,0:T(8,128)S(1)} %get-tuple-element.62, ...), kind=kOutput, calls=%fused_computation.83 | convolution fusion | flops 53477376 | bytes 661504 | tf_op jit(solution)/shard_map/njkm,njmr->nkr/dot_general | solution.py:63
  251.1 2.4 convolution_bitcast_fusion.3
  254.5 0.8 pad_maximum_fusion.2
  255.3 0.8 gather_fusion.6
  256.7 0.7 slice_bitcast_fusion.6
  257.4 0.7 reshape.350
  258.1 5.7 %fusion.81 = f32[16,32,16]{1,2,0:T(8,128)S(1)} fusion(f32[16,8,32,16]{3,2,1,0:T(8,128)S(1)} %reshape.350, f32[16,8,32]{2,1,0:T(8,128)} %get-tuple-element.66, f32[16,32]{1,0:T(8,128)S(1)} %get-tuple-element.75, f32[16,8,32]{2,1,0:T(8,128)} %get-tuple-element.67, f32[16,32]{1,0:T(8,128)} %get-tuple-element.76, f32[16,8,32]{2,1,0:T(8,128)} %get-tuple-element.65, ...), kind=kOutput, calls=%fused_computation.91 | convolution fusion | flops 26738688 | bytes 350208 | tf_op jit(solution)/shard_map/njkm,njmr->nkr/dot_general | solution.py:63
  264.7 18.2 %while.10 = (s32[]{:T(128)}, f32[2,16,8,128]{3,1,2,0:T(8,128)S(1)}, s32[2]{0:T(128)S(1)}, s32[16,16]{1,0:T(8,128)S(1)}, f32[19,48,128]{2,0,1:T(8,128)S(1)}, /*in...) while((s32[]{:T(128)}, f32[2,16,8,128]{3,1,2,0:T(8,128)S(1)}, ...), condition=%wide.region_2.3_spmd, body=%wide.region_1.2_spmd.sunk | while | flops 213911856 | bytes 2398031 | solution.py:146
  267.8 6.2 %fusion.187 = f32[2,16,8,128]{3,1,2,0:T(8,128)S(1)} fusion(f32[2,16,8,128]{3,1,2,0:T(8,128)S(1)} %get-tuple-element.144, s32[]{:T(128)} %get-tuple-element.143, f32[8,8,128]{2,1,0:T(8,128)S(1)} %bitcast.200, f32[8,128]{1,0:T(8,128)S(1)} %bitcast.208, f32[8,8,128]{2,1,0:T(8,128)S(1)} %bitcast.201, f32[8,128]{1,0:T(8,128)S(1)} %bitcast.209, ...), kind=kOutput, calls=%fused_computation.32.clone.1 | convolution fusion | flops 213909504 | bytes 700420 | tf_op jit(solution)/shard_map/while/body/eval_jaxpr/bjpq,rbjq->rbp/dot_general | solution.py:144
  276.8 6.2 %fusion.187 = f32[2,16,8,128]{3,1,2,0:T(8,128)S(1)} fusion(f32[2,16,8,128]{3,1,2,0:T(8,128)S(1)} %get-tuple-element.144, s32[]{:T(128)} %get-tuple-element.143, f32[8,8,128]{2,1,0:T(8,128)S(1)} %bitcast.200, f32[8,128]{1,0:T(8,128)S(1)} %bitcast.208, f32[8,8,128]{2,1,0:T(8,128)S(1)} %bitcast.201, f32[8,128]{1,0:T(8,128)S(1)} %bitcast.209, ...), kind=kOutput, calls=%fused_computation.32.clone.1 | convolution fusion | flops 213909504 | bytes 700420 | tf_op jit(solution)/shard_map/while/body/eval_jaxpr/bjpq,rbjq->rbp/dot_general | solution.py:144
  283.3 0.7 copy.92
  (125 shorter events, 12.1 us)
Async XLA Ops:
  0.0 1.0 copy-start
  0.0 176.6 %copy-start.9 = (s32[16,16]{1,0:T(8,128)S(1)}, s32[16,16]{1,0:T(8,128)}, u32[]{:S(2)}) copy-start(s32[16,16]{1,0:T(8,128)} %param.31) | copy-start | bytes 3076
  3.4 251.0 %collective-permute-start = (f32[16,516]{1,0:T(8,128)S(1)}, f32[16,516]{1,0:T(8,128)}, u32[]{:S(2)}, u32[]{:S(2)}) collective-permute-start(f32[16,516]{1,0:T(8,128)S(1)} %pad_maximum_fusion.4), channel_id=1, source_target_pairs={{0,1},{1,2},{2,3},{3,4},{4,5},{5,6},{6,7},{7,8},{8,9},{9,10},{10,1... | collective-permute-start | bytes 99080 | tf_op jit(solution)/shard_map/ppermute | solution.py:24
  6.8 247.6 %collective-permute-start.1 = (f32[16,516]{1,0:T(8,128)S(1)}, f32[16,516]{1,0:T(8,128)}, u32[]{:S(2)}, u32[]{:S(2)}) collective-permute-start(f32[16,516]{1,0:T(8,128)S(1)} %pad_maximum_fusion.4), channel_id=1, source_target_pairs={{1,0},{2,1},{3,2},{4,3},{5,4},{6,5},{7,6},{8,7},{9,8},{10,9},{11,1... | collective-permute-start | bytes 99080 | tf_op jit(solution)/shard_map/ppermute | solution.py:27
  13.9 250.5 %collective-permute-start.2 = (f32[19,2048]{1,0:T(8,128)S(1)}, f32[19,2048]{1,0:T(8,128)S(1)}, u32[]{:S(2)}, u32[]{:S(2)}) collective-permute-start(f32[19,2048]{1,0:T(8,128)S(1)} %pad_maximum_fusion.1), channel_id=1, source_target_pairs={{0,1},{1,2},{2,3},{3,4},{4,5},{5,6},{6,7},{7,8},{8,9},{9,10},{10,1... | collective-permute-start | bytes 466952 | tf_op jit(solution)/shard_map/ppermute | solution.py:24
  15.8 248.6 %collective-permute-start.3 = (f32[19,2048]{1,0:T(8,128)S(1)}, f32[19,2048]{1,0:T(8,128)S(1)}, u32[]{:S(2)}, u32[]{:S(2)}) collective-permute-start(f32[19,2048]{1,0:T(8,128)S(1)} %pad_maximum_fusion.1), channel_id=1, source_target_pairs={{1,0},{2,1},{3,2},{4,3},{5,4},{6,5},{7,6},{8,7},{9,8},{10,9},{11,1... | collective-permute-start | bytes 466952 | tf_op jit(solution)/shard_map/ppermute | solution.py:27
  24.1 153.9 %copy-start.6 = (f32[16,4]{0,1:T(4,128)S(1)}, f32[16,4]{0,1:T(4,128)}, u32[]{:S(2)}) copy-start(f32[16,4]{0,1:T(4,128)} %param.21) | copy-start | bytes 772
  24.1 153.9 %copy-start.7 = (f32[16,4]{0,1:T(4,128)S(1)}, f32[16,4]{0,1:T(4,128)}, u32[]{:S(2)}) copy-start(f32[16,4]{0,1:T(4,128)} %param.30) | copy-start | bytes 772
  26.6 151.5 %copy-start.12 = (s32[1,8]{1,0:T(1,128)S(1)}, s32[1,8]{1,0:T(1,128)}, u32[]{:S(2)}) copy-start(s32[1,8]{1,0:T(1,128)} %param.26) | copy-start | bytes 100
  26.7 151.6 %copy-start.8 = (f32[8,4]{0,1:T(4,128)S(1)}, f32[8,4]{0,1:T(4,128)}, u32[]{:S(2)}) copy-start(f32[8,4]{0,1:T(4,128)} %param.25) | copy-start | bytes 388
  176.6 56.4 %copy-start.10 = (s32[8,8]{1,0:T(8,128)S(1)}, s32[8,8]{1,0:T(8,128)}, u32[]{:S(2)}) copy-start(s32[8,8]{1,0:T(8,128)} %param.29) | copy-start | bytes 772
  176.6 56.4 %copy-start.11 = (s32[8,8]{1,0:T(8,128)S(1)}, s32[8,8]{1,0:T(8,128)}, u32[]{:S(2)}) copy-start(s32[8,8]{1,0:T(8,128)} %param.28) | copy-start | bytes 772
  176.8 57.1 %copy-start.13 = (s32[1,16]{1,0:T(1,128)S(1)}, s32[1,16]{1,0:T(1,128)}, u32[]{:S(2)}) copy-start(s32[1,16]{1,0:T(1,128)} %param.23) | copy-start | bytes 196
  233.8 5.0 %copy-start.5 = (s32[16,16]{1,0:T(8,128)S(1)}, s32[16,16]{1,0:T(8,128)}, u32[]{:S(2)}) copy-start(s32[16,16]{1,0:T(8,128)} %param.22) | copy-start | bytes 3076
  250.5 3.0 %copy-start.2 = (f32[8,32,32]{2,1,0:T(8,128)S(1)}, f32[8,32,32]{2,1,0:T(8,128)}, u32[]{:S(2)}) copy-start(f32[8,32,32]{2,1,0:T(8,128)} %param.27) | copy-start | bytes 98308
  258.1 5.7 %copy-start.1 = (f32[16,32,32]{2,1,0:T(8,128)S(1)}, f32[16,32,32]{2,1,0:T(8,128)}, u32[]{:S(2)}) copy-start(f32[16,32,32]{2,1,0:T(8,128)} %param.24) | copy-start | bytes 196612
  258.1 6.2 %copy-start.3 = (f32[3,2048]{1,0:T(4,128)S(1)}, f32[3,2048]{1,0:T(4,128)}, u32[]{:S(2)}) copy-start(f32[3,2048]{1,0:T(4,128)} %param.17) | copy-start | bytes 73732
  263.8 1.0 copy-start.4
where the time goes:
time: 285 us; the launch traced here: 284 us
  blocking collectives  204 us (72%)
  matrix products  38.4 us (13%)
  local copies, waits for them, and re-layouts  19.3 us (7%)
  starting transfers between devices  15.9 us (6%)
  other arithmetic  4.5 us (2%)
    psum x1, blocking collectives, on_device(): coeff_top = lax.psum(partial_top, 'leaf')  136 us
    all_gather x1, blocking collectives, on_device(): mid_all = lax.all_gather(mid_rows, 'leaf', axis=0, tiled=True)  54.6 us
    dot_general x3, matrix products, couple_rows(): jnp.einsum('njkm,njmr->nkr', coupling, source_coeff, precision=exact_prod...  19 us
    all_gather x1, blocking collectives, on_device(): top_all = lax.all_gather(top_rows, 'group', axis=0, tiled=True)  13.4 us
    dot_general x2, matrix products, near_block(): jnp.einsum('bjpq,rbjq->rbp', kernel, source[:RHS], precision=exact_product)  12.4 us
    ppermute x2, starting transfers between devices, extended(): lax.ppermute(lax.slice_in_dim(block, 0, width, axis=dim), axis, backward)  10.6 us
  transfers between devices with their start and end apart: 4, of which 0 were waited for; matrix products, arithmetic and copies ran while one was open for 14% of the time, Pallas kernels for 0%

commit v1 on v0

v1 whole, which is shorter than its diff:
```python
import functools

import jax
import jax.numpy as jnp
import numpy as np
from jax import lax
from jax.experimental import pallas as pl
from jax.experimental.pallas import tpu as pltpu
from jax.sharding import PartitionSpec as P

MESH = pl.DeviceIdType.MESH
HI = lax.Precision.HIGHEST
PTS = 128
RANK = 32
RHS = 16
RATE = 1.7320508075688772 / 0.5
NX = 4
NZ = 8
NL = 32
NG = 8


def node_table():
    k = np.arange(RANK)
    rows = [
        np.cos(np.pi * (((k * (2 * d + 3)) % RANK) + 0.5) / RANK) for d in range(3)
    ]
    return np.stack(rows).astype(np.float32)


def nt(a, b, precision=HI):
    return lax.dot_general(
        a,
        b,
        (((1,), (1,)), ((), ())),
        precision=precision,
        preferred_element_type=jnp.float32,
    )


def nn(a, b):
    return lax.dot_general(
        a,
        b,
        (((1,), (0,)), ((), ())),
        precision=HI,
        preferred_element_type=jnp.float32,
    )


def kappa(squared):
    squared = jnp.maximum(squared, 1e-30)
    t = squared * lax.rsqrt(squared)
    return (1.0 + t) * jnp.exp(-t)


def block_of(shape):
    return lax.broadcasted_iota(jnp.int32, shape, 1) >> 5


def up_kernel(counts, owner, parent, rhs, basis, leaf_t, mid_t, masked, leafc, midc, ptop):
    lane = lax.broadcasted_iota(jnp.int32, (RHS, PTS), 1)
    pieces = []
    for l in range(16):
        cols = slice(l * PTS, (l + 1) * PTS)
        m = jnp.where(lane < counts[l], rhs[:, cols], 0.0)
        masked[:, cols] = m
        pieces.append(nt(m, basis[l]))
    row = lax.broadcasted_iota(jnp.int32, (128, 128), 0) >> 4
    blk = block_of((128, 128))
    total = jnp.zeros((128, RANK), jnp.float32)
    for q in range(4):
        tile = jnp.concatenate(pieces[4 * q : 4 * q + 4], axis=1)
        leafc[q] = tile
        own = jnp.full((128, 128), owner[0, 4 * q], jnp.int32)
        for b in range(1, 4):
            own = jnp.where(blk == b, owner[0, 4 * q + b], own)
        lhs = jnp.where(own == row, jnp.concatenate([tile] * 8, axis=0), 0.0)
        total = total + nn(lhs, leaf_t[4 * q : 4 * q + 4].reshape(128, RANK))
    row = lax.broadcasted_iota(jnp.int32, (256, 128), 0) >> 4
    blk = block_of((256, 128))
    tops = jnp.zeros((256, RANK), jnp.float32)
    for q in range(2):
        tile = jnp.concatenate(
            [total[(4 * q + b) * 16 : (4 * q + b + 1) * 16] for b in range(4)], axis=1
        )
        midc[q] = tile
        own = jnp.full((256, 128), parent[0, 4 * q], jnp.int32)
        for b in range(1, 4):
            own = jnp.where(blk == b, parent[0, 4 * q + b], own)
        lhs = jnp.where(own == row, jnp.concatenate([tile] * 16, axis=0), 0.0)
        tops = tops + nn(lhs, mid_t[4 * q : 4 * q + 4].reshape(128, RANK))
    for q in range(4):
        tile = jnp.concatenate(
            [tops[(4 * q + b) * 16 : (4 * q + b + 1) * 16] for b in range(4)], axis=1
        )
        for i in range(8):
            ptop[q * 8 + i] = tile[2 * i : 2 * i + 2]


def comm_kernel(
    masked, points, leafc, midc, ptop, geo, tgeo,
    mhalo, phalo, lhalo, mids, geos, tgeos, tops,
    rsbuf, zbuf,
    s_rs, r_rs, s_h, r_h, s_mid, r_mid, s_geo, r_geo, s_tg, r_tg, s_z, r_z, s_top, r_top,
):
    g = lax.axis_index("group")
    d = lax.axis_index("leaf")
    z = d // NX
    x = d % NX

    def leaf_peer(k):
        return (g, lax.rem(d + k, NL))

    def ring_peer(k):
        return (g, lax.rem(z + k, NZ) * NX + x)

    def plane_peer(k):
        return (lax.rem(g + k // NX, NG), z * NX + lax.rem(x + k % NX, NX))

    barrier = pltpu.get_barrier_semaphore()

    def hello_leaf(k, c):
        pl.semaphore_signal(barrier, inc=1, device_id=leaf_peer(k), device_id_type=MESH)
        return c

    def hello_plane(k, c):
        pl.semaphore_signal(barrier, inc=1, device_id=plane_peer(k), device_id_type=MESH)
        return c

    lax.fori_loop(1, NL, hello_leaf, 0)
    lax.fori_loop(1, 32, hello_plane, 0)
    pl.semaphore_wait(barrier, 62)

    def copy(src, dst, ss, rs, peer):
        return pltpu.make_async_remote_copy(
            src_ref=src, dst_ref=dst, send_sem=ss, recv_sem=rs, device_id=peer, device_id_type=MESH
        )

    def rs_copy(k):
        o = lax.rem(d + k, NL)
        return copy(
            ptop.at[(o % NX) * 8 + o // NX], rsbuf.at[k], s_rs.at[k], r_rs.at[k], leaf_peer(k)
        )

    def geo_copy(k):
        return copy(geo, geos.at[d], s_geo.at[k], r_geo.at[k], leaf_peer(k))

    def mid_copy(k):
        return copy(midc, mids.at[d], s_mid.at[k], r_mid.at[k], leaf_peer(k))

    def tg_copy(k):
        return copy(tgeo, tgeos.at[g], s_tg.at[k], r_tg.at[k], (lax.rem(g + k, NG), d))

    def z_copy(k):
        return copy(zbuf.at[z], zbuf.at[z], s_z.at[k], r_z.at[k], ring_peer(k))

    def top_copy(k):
        return copy(zbuf, tops.at[g * NX + x], s_top.at[k], r_top.at[k], plane_peer(k))

    halo = []
    for side in range(2):
        peer = leaf_peer(NL - 1 if side == 0 else 1)
        slot = 1 - side
        halo.append(copy(points, phalo.at[slot], s_h.at[slot, 0], r_h.at[slot, 0], peer))
        halo.append(copy(masked, mhalo.at[slot], s_h.at[slot, 1], r_h.at[slot, 1], peer))
        halo.append(copy(leafc, lhalo.at[slot], s_h.at[slot, 2], r_h.at[slot, 2], peer))

    def each(lo, hi, f):
        def step(k, c):
            f(k)
            return c

        lax.fori_loop(lo, hi, step, 0)

    each(1, NL, lambda k: rs_copy(k).start())
    each(1, NL, lambda k: geo_copy(k).start())
    each(1, NG, lambda k: tg_copy(k).start())
    for c in halo:
        c.start()
    mids[d] = midc[...]
    geos[d] = geo[...]
    tgeos[g] = tgeo[...]
    each(1, NL, lambda k: rs_copy(k).wait_recv())
    total = ptop[x * 8 + z]
    for k in range(1, NL):
        total = total + rsbuf[k]
    zbuf[z] = total
    each(1, NZ, lambda k: z_copy(k).start())
    each(1, NL, lambda k: mid_copy(k).start())
    each(1, NZ, lambda k: z_copy(k).wait_recv())
    each(1, 32, lambda k: top_copy(k).start())
    tops[g * NX + x] = zbuf[...]
    each(1, NL, lambda k: mid_copy(k).wait_recv())
    each(1, NL, lambda k: geo_copy(k).wait_recv())
    each(1, NG, lambda k: tg_copy(k).wait_recv())
    for c in halo:
        c.wait_recv()
    each(1, 32, lambda k: top_copy(k).wait_recv())
    each(1, NL, lambda k: rs_copy(k).wait_send())
    each(1, NL, lambda k: geo_copy(k).wait_send())
    each(1, NG, lambda k: tg_copy(k).wait_send())
    each(1, NZ, lambda k: z_copy(k).wait_send())
    each(1, NL, lambda k: mid_copy(k).wait_send())
    each(1, 32, lambda k: top_copy(k).wait_send())
    for c in halo:
        c.wait_send()


def down_kernel(
    counts, owner, parent, partners, peers, slots, offsets, geos, tgeos,
    masked, points, leafc, mhalo, phalo, lhalo, mids, tops, basis, leaf_t, mid_t, trow, tcol,
    out,
    mhl, pts, lwin, mid_s, tb, far_s,
):
    g = lax.axis_index("group")
    d = lax.axis_index("leaf")
    blk16 = block_of((RHS, 128))
    blk1 = block_of((1, 128))

    def gather(tab, srcs):
        acc = None
        for j, s in enumerate(srcs):
            t = pltpu.roll(tab[s >> 2], ((j - (s & 3)) & 3) * 32, 1)
            acc = t if j == 0 else jnp.where(blk16 == j, t, acc)
        return acc

    def target_nodes(read):
        h = read(3)
        return [(read(c) + h * tcol[c]) * RATE for c in range(3)]

    def coupling(tnodes, reads):
        def mix(c):
            v = jnp.full((1, 128), reads[0](c), jnp.float32)
            for j in range(1, 4):
                v = jnp.where(blk1 == j, reads[j](c), v)
            return v

        h = mix(3)
        squared = None
        for c in range(3):
            row = (mix(c) + h * trow[c : c + 1, :]) * RATE
            diff = tnodes[c] - row
            squared = diff * diff if squared is None else squared + diff * diff
        return kappa(squared)

    def top_read(s):
        return lambda c: tgeos[s >> 4, c * 16 + (s & 15)]

    def mid_read(i):
        return lambda c: geos[i >> 3, c * 8 + (i & 7)]

    def leaf_read(w):
        dev = lax.rem(d + NL - 1 + (w >> 4), NL)
        return lambda c: geos[dev, 32 + c * 16 + (w & 15)]

    def window(i, carry):
        cols = pl.ds(pl.multiple_of(i * PTS, PTS), PTS)
        for part in range(3):
            if part == 1:
                m, p = masked[:, cols], points[:, cols]
            else:
                m, p = mhalo[part // 2, :, cols], phalo[part // 2, :, cols]
            high = m.astype(jnp.bfloat16)
            low = (m - high.astype(jnp.float32)).astype(jnp.bfloat16)
            mhl[part * 16 + i] = jnp.concatenate([high, low], axis=0)
            pts[part * 16 + i, 0:3] = p * RATE
        return carry

    pts[...] = jnp.zeros_like(pts)
    lax.fori_loop(0, 16, window, 0)
    lwin[0:4] = lhalo[0]
    lwin[4:8] = leafc[...]
    lwin[8:12] = lhalo[1]

    def mid_step(b, carry):
        p = parent[0, b]
        t = g * 16 + p
        nodes = target_nodes(top_read(t))
        cs, ss = [], []
        for q in range(4):
            srcs = [(t + offsets[p, 4 * q + j]) & 127 for j in range(4)]
            cs.append(gather(tops, srcs))
            ss.append(coupling(nodes, [top_read(s) for s in srcs]))
        local = nt(jnp.concatenate(cs, axis=1), jnp.concatenate(ss, axis=1))
        nodes = target_nodes(mid_read(d * 8 + b))
        cs, ss = [], []
        for q in range(2):
            srcs = [peers[b, 4 * q + j] * 8 + slots[b, 4 * q + j] for j in range(4)]
            cs.append(gather(mids, srcs))
            ss.append(coupling(nodes, [mid_read(s) for s in srcs]))
        mid_s[b] = nt(local, mid_t[b]) + nt(
            jnp.concatenate(cs, axis=1), jnp.concatenate(ss, axis=1)
        )
        return carry

    lax.fori_loop(0, 8, mid_step, 0)

    def leaf_step(l, carry):
        nodes = target_nodes(leaf_read(l + 16))
        cs, ss = [], []
        for q in range(2):
            srcs = [l + 16 + partners[l, 8 + 4 * q + j] for j in range(4)]
            cs.append(gather(lwin, srcs))
            ss.append(coupling(nodes, [leaf_read(s) for s in srcs]))
        local = nt(mid_s[owner[0, l]], leaf_t[l]) + nt(
            jnp.concatenate(cs, axis=1), jnp.concatenate(ss, axis=1)
        )
        far_s[l] = nn(local, basis[l])
        return carry

    lax.fori_loop(0, 16, leaf_step, 0)
    lane = lax.broadcasted_iota(jnp.int32, (RHS, PTS), 1)

    def near_step(l, carry):
        target = pts[l + 16].T
        for c in range(3):
            tb[c] = jnp.broadcast_to(target[:, c : c + 1], (PTS, PTS))
        both = jnp.zeros((PTS, 2 * RHS), jnp.float32)
        rest = jnp.zeros((PTS, RHS), jnp.float32)
        for j in range(0, 8, 2):
            highs, lows, ms = [], [], []
            for e in range(2):
                w = l + 16 + partners[l, j + e]
                squared = None
                for c in range(3):
                    diff = tb[c] - pts[w, c : c + 1, :]
                    squared = diff * diff if squared is None else squared + diff * diff
                k = kappa(squared)
                high = k.astype(jnp.bfloat16)
                highs.append(high)
                lows.append((k - high.astype(jnp.float32)).astype(jnp.bfloat16))
                ms.append(mhl[w])
            m = jnp.concatenate(ms, axis=1)
            both = both + nt(jnp.concatenate(highs, axis=1), m, None)
            rest = rest + nt(jnp.concatenate(lows, axis=1), m[:RHS], None)
        near = both[:, :RHS] + both[:, RHS:] + rest
        cols = pl.ds(pl.multiple_of(l * PTS, PTS), PTS)
        out[:, cols] = jnp.where(lane < counts[l], near.T + far_s[l], 0.0)
        return carry

    lax.fori_loop(0, 16, near_step, 0)


VM = pl.BlockSpec(memory_space=pltpu.VMEM)
SM = pl.BlockSpec(memory_space=pltpu.SMEM)


def f32(*shape):
    return jax.ShapeDtypeStruct(shape, jnp.float32)


def on_device(
    points, rhs, counts, basis, leaf_geom, leaf_partners, leaf_middle_owner, leaf_basis_transfer,
    mid_geom, mid_parent, mid_transfer, mid_peers, mid_slots, top_geom, top_offsets,
):
    basis_t = jnp.swapaxes(basis, 1, 2)
    masked, leafc, midc, ptop = pl.pallas_call(
        up_kernel,
        out_shape=(f32(16, 2048), f32(4, 16, 128), f32(2, 16, 128), f32(32, 2, 128)),
        in_specs=[SM] * 3 + [VM] * 4,
        out_specs=(VM,) * 4,
        name="up",
    )(counts, leaf_middle_owner, mid_parent, rhs, basis_t, leaf_basis_transfer, mid_transfer)
    geo = jnp.concatenate(
        [mid_geom.T.reshape(32), leaf_geom.T.reshape(64), jnp.zeros((32,), jnp.float32)]
    )[None]
    tgeo = jnp.concatenate([top_geom.T.reshape(64), jnp.zeros((64,), jnp.float32)])[None]
    dma = pltpu.SemaphoreType.DMA
    mhalo, phalo, lhalo, mids, geos, tgeos, tops = pl.pallas_call(
        comm_kernel,
        out_shape=(
            f32(2, 16, 2048), f32(2, 3, 2048), f32(2, 4, 16, 128), f32(32, 2, 16, 128),
            f32(32, 1, 128), f32(8, 1, 128), f32(32, 8, 2, 128),
        ),
        in_specs=[VM] * 7,
        out_specs=(VM,) * 7,
        scratch_shapes=[
            pltpu.VMEM((32, 2, 128), jnp.float32),
            pltpu.VMEM((8, 2, 128), jnp.float32),
            dma((32,)), dma((32,)), dma((2, 3)), dma((2, 3)), dma((32,)), dma((32,)),
            dma((32,)), dma((32,)), dma((8,)), dma((8,)), dma((8,)), dma((8,)),
            dma((32,)), dma((32,)),
        ],
        compiler_params=pltpu.CompilerParams(collective_id=0, has_side_effects=True),
        name="exchange",
    )(masked, points, leafc, midc, ptop, geo, tgeo)
    table = node_table()
    trow = np.zeros((8, 128), np.float32)
    trow[:3] = np.tile(table, (1, 4))
    tcol = np.broadcast_to(table[:, :, None], (3, 32, 128)).astype(np.float32)
    return pl.pallas_call(
        down_kernel,
        out_shape=f32(16, 2048),
        in_specs=[SM] * 9 + [VM] * 13,
        out_specs=VM,
        scratch_shapes=[
            pltpu.VMEM((48, 32, 128), jnp.bfloat16),
            pltpu.VMEM((48, 8, 128), jnp.float32),
            pltpu.VMEM((12, 16, 128), jnp.float32),
            pltpu.VMEM((8, 16, 32), jnp.float32),
            pltpu.VMEM((3, 128, 128), jnp.float32),
            pltpu.VMEM((16, 16, 128), jnp.float32),
        ],
        name="down",
    )(
        counts, leaf_middle_owner, mid_parent, leaf_partners, mid_peers, mid_slots, top_offsets,
        geos.reshape(32, 128), tgeos.reshape(8, 128),
        masked, points, leafc, mhalo, phalo, lhalo, mids.reshape(64, 16, 128),
        tops.reshape(32, 16, 128), basis_t, leaf_basis_transfer, mid_transfer,
        jnp.asarray(trow), jnp.asarray(tcol),
    )


def solution(mesh):
    both = ("group", "leaf")
    placed = (
        P(None, both), P(None, both), P(both), P(both, None, None), P(both, None), P(both, None),
        P(both, None), P(both, None, None), P(both, None), P("group", "leaf"), P(both, None, None),
        P(both, None), P(both, None), P("group", None), P("group", None),
    )
    return jax.shard_map(
        on_device, mesh=mesh, in_specs=placed, out_specs=P(None, both), check_vma=False
    )
```

time: 285 us -> 67.9 us (0.24)
  the two profiles are of different devices: /device:TPU:32 before, /device:TPU:1 now
where the time goes in v1:
time: 67.9 us; the launch traced here: 67.2 us
  Pallas kernels  65.1 us (96%)
  local copies, waits for them, and re-layouts  1.44 us (2%)
    pallas_call x1, Pallas kernels, on_device(): pl.pallas_call(comm_kernel, out_shape=(f32(2, 16, 2048), f32(2, 3, 2048),...  35.9 us
    pallas_call x1, Pallas kernels, on_device(): pl.pallas_call(down_kernel, out_shape=f32(16, 2048), in_specs=[SM] * 9 +...  25.8 us
    pallas_call x1, Pallas kernels, on_device(): pl.pallas_call(up_kernel, out_shape=(f32(16, 2048), f32(4, 16, 128), f32(...  3.36 us

profile of v1, /device:TPU:1, one launch (start us, length us, event | category | flops | bytes accessed | tf_op | source)
XLA Modules:
  0.0 67.2 jit_solution(5562401343653981493)
XLA Ops:
  0.0 0.0 copy-start
  0.0 0.0 copy-start.1
  0.0 0.7 %copy-done = f32[16,4]{0,1:T(4,128)S(1)} copy-done((f32[16,4]{0,1:T(4,128)S(1)}, f32[16,4]{0,1:T(4,128)}, u32[]{:S(2)}) %copy-start) | copy-done | bytes 280
  0.7 0.0 copy-start.2
  0.7 0.1 reshape.22
  0.8 0.0 copy-done.1
  0.8 0.1 reshape.21
  0.9 0.5 copy-done.2
  1.4 0.1 reshape.23
  1.4 0.7 maximum_bitcast_fusion
  2.1 3.4 %up.1 = (f32[16,2048]{1,0:T(8,128)}, f32[4,16,128]{2,1,0:T(8,128)}, f32[2,16,128]{2,1,0:T(8,128)}, f32[32,2,128]{2,1,0:T(2,128)}) custom-call(s32[16]{0:T(128)} %counts.3, s32[1,16]{1,0:T(1,128)} %owner.3, s32[1,8]{1,0:T(1,128)} %parent.3, f32[16,2048]{1,0:T(8,128)} %rhs.1, f32[16,32,128]{2,1,0:T(8,128)} %bitcast.12, f32[16,32,32]{2,1,0:T(8,128)} %leaf_t.3, ...), custom_call_target="tpu_custom_call" | custom-call | tf_op jit(solution)/shard_map/up/pallas_call | solution.py:358
  5.5 35.9 %exchange.1 = (f32[2,16,2048]{2,1,0:T(8,128)}, f32[2,3,2048]{2,1,0:T(4,128)}, f32[2,4,16,128]{3,2,1,0:T(8,128)}, f32[32,2,16,128]{3,2,1,0:T(8,128)}, f32[32,1,12...) custom-call(f32[16,2048]{1,0:T(8,128)} %get-tuple-element.16.masked, f32[3,2048]{1,0:T(4,128)} %points.3, ...), custom_call_target="tpu_custom_call" | custom-call | tf_op jit(solution)/shard_map/exchange/pallas_call | solution.py:370
  41.4 25.8 %down.1 = f32[16,2048]{1,0:T(8,128)} custom-call(s32[16]{0:T(128)} %counts.3, s32[1,16]{1,0:T(1,128)} %owner.3, s32[1,8]{1,0:T(1,128)} %parent.3, s32[16,16]{1,0:T(8,128)} %partners.1, s32[8,8]{1,0:T(8,128)} %peers.1, s32[8,8]{1,0:T(8,128)} %slots.1, s32[16,16]{1,0:T(8,128)} %offsets.1, f32[32,128]{1,0:T(8,128)} %bitcast.16, f32[8,128]{1,0:T(8,128)} %bitcast.17, ...), custom_call_target="tpu_custom_call" | custom-call | tf_op jit(solution)/shard_map/down/pallas_call | solution.py:392
  (1 shorter events, 0.0 us)
Async XLA Ops:
  0.0 0.7 %copy-start = (f32[16,4]{0,1:T(4,128)S(1)}, f32[16,4]{0,1:T(4,128)}, u32[]{:S(2)}) copy-start(f32[16,4]{0,1:T(4,128)} %param.21) | copy-start | bytes 772
  0.0 0.8 %copy-start.1 = (f32[8,4]{0,1:T(4,128)S(1)}, f32[8,4]{0,1:T(4,128)}, u32[]{:S(2)}) copy-start(f32[8,4]{0,1:T(4,128)} %param.25) | copy-start | bytes 388
  0.7 0.7 %copy-start.2 = (f32[16,4]{0,1:T(4,128)S(1)}, f32[16,4]{0,1:T(4,128)}, u32[]{:S(2)}) copy-start(f32[16,4]{0,1:T(4,128)} %param.30) | copy-start | bytes 772

commit v2 on v1

v2 whole, which is shorter than its diff:
```python
import functools

import jax
import jax.numpy as jnp
import numpy as np
from jax import lax
from jax.experimental import pallas as pl
from jax.experimental.pallas import tpu as pltpu
from jax.sharding import PartitionSpec as P

MESH = pl.DeviceIdType.MESH
HI = lax.Precision.HIGHEST
PTS = 128
RANK = 32
RHS = 16
RATE = 1.7320508075688772 / 0.5
NX = 4
NZ = 8
NL = 32
NG = 8


def node_table():
    k = np.arange(RANK)
    rows = [
        np.cos(np.pi * (((k * (2 * d + 3)) % RANK) + 0.5) / RANK) for d in range(3)
    ]
    return np.stack(rows).astype(np.float32)


def nt(a, b, precision=HI):
    return lax.dot_general(
        a,
        b,
        (((1,), (1,)), ((), ())),
        precision=precision,
        preferred_element_type=jnp.float32,
    )


def nn(a, b):
    return lax.dot_general(
        a,
        b,
        (((1,), (0,)), ((), ())),
        precision=HI,
        preferred_element_type=jnp.float32,
    )


def kappa(squared):
    squared = jnp.maximum(squared, 1e-30)
    t = squared * lax.rsqrt(squared)
    return (1.0 + t) * jnp.exp(-t)


def block_of(shape):
    return lax.broadcasted_iota(jnp.int32, shape, 1) >> 5


def loop(count, width, f):
    def step(i, c):
        for e in range(width):
            f(i * width + e)
        return c

    lax.fori_loop(0, count // width, step, 0)


def whole_kernel(
    counts, owner, parent, partners, peers, slots, offsets, mgeo, lgeo, ggeo,
    points, rhs, basis_h, leaf_h, mid_h, trow, tcol,
    out,
    rhs_s, basis, leaf_t, mid_t, mwin, pwin, lwin, midc, ptop, geo, tgeo,
    mids, geos, tgeos, tops, rsbuf, zbuf, ztile,
    mhl, awin, bwin, base_s, far_m, p_s, w_s, mid_s, geos_v, tgeos_v,
    s_in, s_rs, r_rs, s_h, r_h, s_mid, r_mid, s_geo, r_geo, s_tg, r_tg, s_z, r_z, s_top, r_top,
):
    g = lax.axis_index("group")
    d = lax.axis_index("leaf")
    z = d // NX
    x = d % NX

    def leaf_peer(k):
        return (g, lax.rem(d + k, NL))

    def ring_peer(k):
        return (g, lax.rem(z + k, NZ) * NX + x)

    def plane_peer(k):
        return (lax.rem(g + k // NX, NG), z * NX + lax.rem(x + k % NX, NX))

    def each(lo, hi, f):
        def step(k, c):
            f(k)
            return c

        lax.fori_loop(lo, hi, step, 0)

    barrier = pltpu.get_barrier_semaphore()

    def hello(peer):
        pl.semaphore_signal(barrier, inc=1, device_id=peer, device_id_type=MESH)

    each(1, NL, lambda k: hello(leaf_peer(k)))
    each(1, 32, lambda k: hello(plane_peer(k)))

    loads = [
        pltpu.make_async_copy(a, b, s_in.at[i])
        for i, (a, b) in enumerate(
            [(rhs, rhs_s), (basis_h, basis), (leaf_h, leaf_t), (mid_h, mid_t), (points, pwin.at[1])]
        )
    ]
    for c in loads:
        c.start()

    def copy(src, dst, ss, rs, peer):
        return pltpu.make_async_remote_copy(
            src_ref=src, dst_ref=dst, send_sem=ss, recv_sem=rs, device_id=peer, device_id_type=MESH
        )

    def rs_copy(k):
        o = lax.rem(d + k, NL)
        return copy(
            ptop.at[(o % NX) * 8 + o // NX], rsbuf.at[k], s_rs.at[k], r_rs.at[k], leaf_peer(k)
        )

    def geo_copy(k):
        return copy(geo, geos_v.at[d], s_geo.at[k], r_geo.at[k], leaf_peer(k))

    def mid_copy(k):
        return copy(midc, mids.at[pl.ds(d * 2, 2)], s_mid.at[k], r_mid.at[k], leaf_peer(k))

    def tg_copy(k):
        return copy(tgeo, tgeos_v.at[g], s_tg.at[k], r_tg.at[k], (lax.rem(g + k, NG), d))

    def z_copy(k):
        return copy(zbuf.at[z], zbuf.at[z], s_z.at[k], r_z.at[k], ring_peer(k))

    def top_copy(k):
        return copy(ztile, tops.at[g * NX + x], s_top.at[k], r_top.at[k], plane_peer(k))

    lhalo, phalo = [], []
    for side in range(2):
        peer = leaf_peer(NL - 1 if side == 0 else 1)
        slot = 1 - side
        lhalo.append(
            copy(lwin.at[4:8], lwin.at[0:4] if side == 1 else lwin.at[8:12],
                 s_h.at[slot, 2], r_h.at[slot, 2], peer)
        )
        part = 0 if side == 1 else 2
        phalo.append(copy(pwin.at[1], pwin.at[part], s_h.at[slot, 0], r_h.at[slot, 0], peer))
        phalo.append(copy(mwin.at[1], mwin.at[part], s_h.at[slot, 1], r_h.at[slot, 1], peer))

    lane1 = lax.broadcasted_iota(jnp.int32, (1, 128), 1)
    row = jnp.zeros((1, 128), jnp.float32)
    for c in range(4):
        for i in range(8):
            row = jnp.where(lane1 == c * 8 + i, mgeo[c, i], row)
        for i in range(16):
            row = jnp.where(lane1 == 32 + c * 16 + i, lgeo[c, i], row)
    geo[...] = row
    geos_v[d] = row
    row = jnp.zeros((1, 128), jnp.float32)
    for c in range(4):
        for i in range(16):
            row = jnp.where(lane1 == c * 16 + i, ggeo[c, i], row)
    tgeo[...] = row
    tgeos_v[g] = row

    lane = lax.broadcasted_iota(jnp.int32, (RHS, PTS), 1)
    loads[0].wait()
    loads[1].wait()
    pieces = []
    for l in range(16):
        cols = slice(l * PTS, (l + 1) * PTS)
        m = jnp.where(lane < counts[l], rhs_s[:, cols], 0.0)
        mwin[1, :, cols] = m
        pieces.append(nt(m, basis[l]))
    loads[2].wait()
    loads[3].wait()
    loads[4].wait()
    srow = lax.broadcasted_iota(jnp.int32, (128, 128), 0) >> 4
    blk = block_of((128, 128))
    total = jnp.zeros((128, RANK), jnp.float32)
    for q in range(4):
        tile = jnp.concatenate(pieces[4 * q : 4 * q + 4], axis=1)
        lwin[4 + q] = tile
        own = jnp.full((128, 128), owner[0, 4 * q], jnp.int32)
        for b in range(1, 4):
            own = jnp.where(blk == b, owner[0, 4 * q + b], own)
        lhs = jnp.where(own == srow, jnp.concatenate([tile] * 8, axis=0), 0.0)
        total = total + nn(lhs, leaf_t[4 * q : 4 * q + 4].reshape(128, RANK))
    srow = lax.broadcasted_iota(jnp.int32, (256, 128), 0) >> 4
    blk = block_of((256, 128))
    topp = jnp.zeros((256, RANK), jnp.float32)
    for q in range(2):
        tile = jnp.concatenate(
            [total[(4 * q + b) * 16 : (4 * q + b + 1) * 16] for b in range(4)], axis=1
        )
        midc[q] = tile
        own = jnp.full((256, 128), parent[0, 4 * q], jnp.int32)
        for b in range(1, 4):
            own = jnp.where(blk == b, parent[0, 4 * q + b], own)
        lhs = jnp.where(own == srow, jnp.concatenate([tile] * 16, axis=0), 0.0)
        topp = topp + nn(lhs, mid_t[4 * q : 4 * q + 4].reshape(128, RANK))
    for q in range(4):
        tile = jnp.concatenate(
            [topp[(4 * q + b) * 16 : (4 * q + b + 1) * 16] for b in range(4)], axis=1
        )
        for i in range(8):
            ptop[q * 8 + i] = tile[2 * i : 2 * i + 2]

    pl.semaphore_wait(barrier, 62)
    each(1, NL, lambda k: rs_copy(k).start())
    for c in phalo:
        c.start()
    each(1, NL, lambda k: geo_copy(k).start())
    each(1, NG, lambda k: tg_copy(k).start())
    for c in lhalo:
        c.start()

    def make_w(l):
        w_s[l] = lax.dot_general(
            leaf_t[l], basis[l], (((0,), (0,)), ((), ())), precision=HI,
            preferred_element_type=jnp.float32,
        )

    loop(16, 4, make_w)

    sub = lax.broadcasted_iota(jnp.int32, (8, PTS), 0)

    def split3(v):
        a = v.astype(jnp.bfloat16).astype(jnp.float32)
        r = v - a
        b = r.astype(jnp.bfloat16).astype(jnp.float32)
        return a, b, r - b

    def window(part, i):
        cols = pl.ds(pl.multiple_of(i * PTS, PTS), PTS)
        m = mwin[part, :, cols]
        high = m.astype(jnp.bfloat16)
        low = (m - high.astype(jnp.float32)).astype(jnp.bfloat16)
        w = part * 16 + i
        mhl[w] = jnp.concatenate([high, low], axis=0)
        c = (pwin[part, :, cols] - 0.5) * RATE
        norm = jnp.sum(c * c, axis=0, keepdims=True)
        c8 = jnp.concatenate([c, jnp.zeros((5, PTS), jnp.float32)], axis=0)
        v = jnp.where(sub == 3, norm, jnp.where(sub == 4, 1.0, c8))
        a, b, e = split3(v)
        bwin[w] = jnp.concatenate([a, a, a, b, b, e], axis=0).astype(jnp.bfloat16)
        if part == 1:
            v = jnp.where(sub == 3, 1.0, jnp.where(sub == 4, norm, -2.0 * c8))
            a, b, e = split3(v)
            awin[i] = jnp.concatenate([a, b, e, a, b, a], axis=0).T.astype(jnp.bfloat16)

    loop(16, 2, lambda i: window(1, i))

    def near(l):
        target = awin[l]
        both = jnp.zeros((PTS, 2 * RHS), jnp.float32)
        rest = jnp.zeros((PTS, RHS), jnp.float32)
        for j in range(0, 8, 2):
            ws = [l + 16 + partners[l, j + e] for e in range(2)]
            source = jnp.concatenate([bwin[w] for w in ws], axis=1)
            k = kappa(
                lax.dot_general(
                    target, source, (((1,), (0,)), ((), ())), preferred_element_type=jnp.float32
                )
            )
            high = k.astype(jnp.bfloat16)
            low = (k - high.astype(jnp.float32)).astype(jnp.bfloat16)
            m = jnp.concatenate([mhl[w] for w in ws], axis=1)
            both = both + nt(high, m, None)
            rest = rest + nt(low, m[:RHS], None)
        base_s[l] = (both[:, :RHS] + both[:, RHS:] + rest).T

    def near_range(lo, hi):
        each(lo, hi, near)

    for c in phalo:
        c.wait_recv()
    loop(16, 2, lambda i: window(0, i))
    loop(16, 2, lambda i: window(2, i))
    near_range(0, N1)

    each(1, NL, lambda k: rs_copy(k).wait_recv())
    total = ptop[x * 8 + z]
    for k in range(1, NL):
        total = total + rsbuf[k]
    zbuf[z] = total
    each(1, NZ, lambda k: z_copy(k).start())
    each(1, NL, lambda k: mid_copy(k).start())
    mids[pl.ds(d * 2, 2)] = midc[...]
    near_range(N1, N2)
    each(1, NZ, lambda k: z_copy(k).wait_recv())
    for i in range(8):
        ztile[2 * i : 2 * i + 2] = zbuf[i]
    each(1, 32, lambda k: top_copy(k).start())
    tops[g * NX + x] = ztile[...]
    near_range(N2, 16)

    each(1, NL, lambda k: geo_copy(k).wait_recv())
    each(1, NG, lambda k: tg_copy(k).wait_recv())
    for c in lhalo:
        c.wait_recv()
    to_smem = [
        pltpu.make_async_copy(geos_v, geos, s_in.at[0]),
        pltpu.make_async_copy(tgeos_v, tgeos, s_in.at[1]),
    ]
    for c in to_smem:
        c.start()
    for c in to_smem:
        c.wait()

    blk16 = block_of((RHS, 128))
    blk1 = block_of((1, 128))

    def gather(tab, srcs):
        acc = None
        for j, s in enumerate(srcs):
            t = pltpu.roll(tab[s >> 2], ((j - (s & 3)) & 3) * 32, 1)
            acc = t if j == 0 else jnp.where(blk16 == j, t, acc)
        return acc

    def target_nodes(read):
        h = read(3)
        return [(read(c) + h * tcol[c]) * RATE for c in range(3)]

    def coupling(tnodes, reads):
        def mix(c):
            v = jnp.full((1, 128), reads[0](c), jnp.float32)
            for j in range(1, 4):
                v = jnp.where(blk1 == j, reads[j](c), v)
            return v

        h = mix(3)
        squared = None
        for c in range(3):
            r = (mix(c) + h * trow[c : c + 1, :]) * RATE
            diff = tnodes[c] - r
            squared = diff * diff if squared is None else squared + diff * diff
        return kappa(squared)

    def top_read(s):
        return lambda c: tgeos[s >> 4, 0, c * 16 + (s & 15)]

    def mid_read(i):
        return lambda c: geos[i >> 3, 0, c * 8 + (i & 7)]

    def leaf_read(w):
        dev = lax.rem(d + NL - 1 + (w >> 4), NL)
        return lambda c: geos[dev, 0, 32 + c * 16 + (w & 15)]

    def leaf_far(l):
        nodes = target_nodes(leaf_read(l + 16))
        cs, ss = [], []
        for q in range(2):
            srcs = [l + 16 + partners[l, 8 + 4 * q + j] for j in range(4)]
            cs.append(gather(lwin, srcs))
            ss.append(coupling(nodes, [leaf_read(s) for s in srcs]))
        local = nt(jnp.concatenate(cs, axis=1), jnp.concatenate(ss, axis=1))
        base_s[l] += nn(local, basis[l])

    loop(16, 2, leaf_far)

    def top_sources(b):
        p = parent[0, b]
        t = g * 16 + p
        return t, [[(t + offsets[p, 4 * q + j]) & 127 for j in range(4)] for q in range(4)]

    def top_coupling(b):
        t, srcs = top_sources(b)
        nodes = target_nodes(top_read(t))
        s = [coupling(nodes, [top_read(i) for i in four]) for four in srcs]
        p_s[b] = nn(mid_t[b], jnp.concatenate(s, axis=1))

    loop(8, 2, top_coupling)

    each(1, NL, lambda k: mid_copy(k).wait_recv())

    def mid_coupling(b):
        nodes = target_nodes(mid_read(d * 8 + b))
        cs, ss = [], []
        for q in range(2):
            srcs = [peers[b, 4 * q + j] * 8 + slots[b, 4 * q + j] for j in range(4)]
            cs.append(gather(mids, srcs))
            ss.append(coupling(nodes, [mid_read(s) for s in srcs]))
        far_m[b] = nt(jnp.concatenate(cs, axis=1), jnp.concatenate(ss, axis=1))

    loop(8, 2, mid_coupling)

    each(1, 32, lambda k: top_copy(k).wait_recv())

    def down_mid(b):
        _, srcs = top_sources(b)
        c = jnp.concatenate([gather(tops, four) for four in srcs], axis=1)
        mid_s[b] = far_m[b] + nt(c, p_s[b])

    loop(8, 4, down_mid)

    for l in range(16):
        cols = slice(l * PTS, (l + 1) * PTS)
        value = base_s[l] + nn(mid_s[owner[0, l]], w_s[l])
        out[:, cols] = jnp.where(lane < counts[l], value, 0.0)

    each(1, NL, lambda k: rs_copy(k).wait_send())
    each(1, NL, lambda k: geo_copy(k).wait_send())
    each(1, NG, lambda k: tg_copy(k).wait_send())
    each(1, NZ, lambda k: z_copy(k).wait_send())
    each(1, NL, lambda k: mid_copy(k).wait_send())
    each(1, 32, lambda k: top_copy(k).wait_send())
    for c in lhalo + phalo:
        c.wait_send()


N1 = 3
N2 = 9
VM = pl.BlockSpec(memory_space=pltpu.VMEM)
SM = pl.BlockSpec(memory_space=pltpu.SMEM)
ANY = pl.BlockSpec(memory_space=pl.ANY)


def on_device(
    points, rhs, counts, basis, leaf_geom, leaf_partners, leaf_middle_owner, leaf_basis_transfer,
    mid_geom, mid_parent, mid_transfer, mid_peers, mid_slots, top_geom, top_offsets,
):
    table = node_table()
    trow = np.zeros((8, 128), np.float32)
    trow[:3] = np.tile(table, (1, 4))
    tcol = np.broadcast_to(table[:, :, None], (3, 32, 128)).astype(np.float32)
    dma = pltpu.SemaphoreType.DMA

    def vm(*shape, dtype=jnp.float32):
        return pltpu.VMEM(shape, dtype)

    return pl.pallas_call(
        whole_kernel,
        out_shape=jax.ShapeDtypeStruct((16, 2048), jnp.float32),
        in_specs=[SM] * 10 + [ANY] * 5 + [VM] * 2,
        out_specs=VM,
        scratch_shapes=[
            vm(16, 2048), vm(16, 32, 128), vm(16, 32, 32), vm(8, 32, 32),
            vm(3, 16, 2048), vm(3, 3, 2048), vm(12, 16, 128), vm(2, 16, 128), vm(32, 2, 128),
            vm(1, 128), vm(1, 128),
            vm(64, 16, 128), pltpu.SMEM((32, 1, 128), jnp.float32),
            pltpu.SMEM((8, 1, 128), jnp.float32), vm(32, 16, 128),
            vm(32, 2, 128), vm(8, 2, 128), vm(16, 128),
            vm(48, 32, 128, dtype=jnp.bfloat16), vm(16, 128, 48, dtype=jnp.bfloat16),
            vm(48, 48, 128, dtype=jnp.bfloat16),
            vm(16, 16, 128), vm(8, 16, 32), vm(8, 32, 512), vm(16, 32, 128), vm(8, 16, 32),
            vm(32, 1, 128), vm(8, 1, 128),
            dma((5,)),
            dma((32,)), dma((32,)), dma((2, 3)), dma((2, 3)), dma((32,)), dma((32,)),
            dma((32,)), dma((32,)), dma((8,)), dma((8,)), dma((8,)), dma((8,)),
            dma((32,)), dma((32,)),
        ],
        compiler_params=pltpu.CompilerParams(collective_id=0, has_side_effects=True),
        name="whole",
    )(
        counts, leaf_middle_owner, mid_parent, leaf_partners, mid_peers, mid_slots, top_offsets,
        mid_geom.T, leaf_geom.T, top_geom.T,
        points, rhs, jnp.swapaxes(basis, 1, 2), leaf_basis_transfer, mid_transfer,
        jnp.asarray(trow), jnp.asarray(tcol),
    )


def solution(mesh):
    both = ("group", "leaf")
    placed = (
        P(None, both), P(None, both), P(both), P(both, None, None), P(both, None), P(both, None),
        P(both, None), P(both, None, None), P(both, None), P("group", "leaf"), P(both, None, None),
        P(both, None), P(both, None), P("group", None), P("group", None),
    )
    return jax.shard_map(
        on_device, mesh=mesh, in_specs=placed, out_specs=P(None, both), check_vma=False
    )
```

time: 67.9 us -> 53.3 us (0.78)
  Pallas kernels: 65.1 us -> 51.5 us
    pallas_call x3 -> x1, Pallas kernels: 65.1 us -> 51.5 us  [on_device(): pl.pallas_call(whole_kernel, out_shape=jax.ShapeDtypeStruct((16, 2048), j...]
    unnamed x6 -> x1, local copies, waits for them, and re-layouts: 1.2 us -> 1.57 us
where the time goes in v2:
time: 53.3 us; the launch traced here: 53.1 us
  Pallas kernels  51.5 us (97%)
  local copies, waits for them, and re-layouts  1.57 us (3%)
    pallas_call x1, Pallas kernels, on_device(): pl.pallas_call(whole_kernel, out_shape=jax.ShapeDtypeStruct((16, 2048), j...  51.5 us
    unnamed x1, local copies, waits for them, and re-layouts  1.57 us

profile of v2, /device:TPU:1, one launch (start us, length us, event | category | flops | bytes accessed | tf_op | source)
XLA Modules:
  0.0 53.1 jit_solution(16073404913919709484)
XLA Ops:
  0.0 51.5 %whole.1 = f32[16,2048]{1,0:T(8,128)} custom-call(s32[16]{0:T(128)} %counts.1, s32[1,16]{1,0:T(1,128)} %owner.1, s32[1,8]{1,0:T(1,128)} %parent.1, s32[16,16]{1,0:T(8,128)} %partners.1, s32[8,8]{1,0:T(8,128)} %peers.1, s32[8,8]{1,0:T(8,128)} %slots.1, s32[16,16]{1,0:T(8,128)} %offsets.1, f32[4,8]{1,0:T(4,128)} %bitcast.5, f32[4,16]{1,0:T(4,128)} %bitcast.6, ...), custom_call_target="tpu_custom_call" | custom-call | tf_op jit(solution)/shard_map/whole/pallas_call | solution.py:437
  51.5 1.6 %copy.19 = f32[16,2048]{1,0:T(8,128)} copy(f32[16,2048]{1,0:T(8,128)} %whole.1) | data formatting | bytes 262144

commit v3 on v2

v3 whole, which is shorter than its diff:
```python
import functools

import jax
import jax.numpy as jnp
import numpy as np
from jax import lax
from jax.experimental import pallas as pl
from jax.experimental.pallas import tpu as pltpu
from jax.sharding import PartitionSpec as P

MESH = pl.DeviceIdType.MESH
PTS = 128
RANK = 32
RHS = 16
RATE = 1.7320508075688772 / 0.5
NX = 4
NZ = 8
NL = 32
NG = 8


def node_table():
    k = np.arange(RANK)
    rows = [
        np.cos(np.pi * (((k * (2 * d + 3)) % RANK) + 0.5) / RANK) for d in range(3)
    ]
    return np.stack(rows).astype(np.float32)


def bf(a):
    return a.astype(jnp.bfloat16)


def raw(a, b, ca, cb):
    return lax.dot_general(
        a, b, (((ca,), (cb,)), ((), ())), preferred_element_type=jnp.float32
    )


def dot3(a, b, ca, cb):
    ah, bh = bf(a), bf(b)
    al, bl = bf(a - ah.astype(jnp.float32)), bf(b - bh.astype(jnp.float32))
    return raw(ah, bh, ca, cb) + (raw(al, bh, ca, cb) + raw(ah, bl, ca, cb))


def nt(a, b):
    return dot3(a, b, 1, 1)


def nn(a, b):
    return dot3(a, b, 1, 0)


def kappa(squared):
    squared = jnp.maximum(squared, 1e-30)
    t = squared * lax.rsqrt(squared)
    return (1.0 + t) * jnp.exp(-t)


def block_of(shape):
    return lax.broadcasted_iota(jnp.int32, shape, 1) >> 5


def loop(count, width, f):
    def step(i, c):
        for e in range(width):
            f(i * width + e)
        return c

    lax.fori_loop(0, count // width, step, 0)


def mask_kernel(counts, product, out):
    lane = lax.broadcasted_iota(jnp.int32, (RHS, PTS), 1)
    for l in range(16):
        cols = slice(l * PTS, (l + 1) * PTS)
        out[:, cols] = jnp.where(lane < counts[l], product[:, cols], 0.0)


def whole_kernel(
    counts_h, owner_h, parent_h, partners_h, peers_h, slots_h, offsets_h, mgeo_h, lgeo_h, ggeo_h,
    points, rhs, basis_h, leaf_h, mid_h, trow_h, tcol_h,
    out,
    counts, owner, parent, partners, peers, slots, offsets, mgeo, lgeo, ggeo, trow, tcol,
    rhs_s, basis, leaf_t, mid_t, mwin, pwin, lwin, midc, ptop, geo, tgeo,
    mids, geos, tgeos, tops, rsbuf, zbuf, ztile,
    mhl, pts, tb, kb0, kb1, base_s, far_m, p_s, w_s, mid_s, geos_v, tgeos_v,
    s_in, sends, recvs,
):
    g = lax.axis_index("group")
    d = lax.axis_index("leaf")
    z = d // NX
    x = d % NX

    def leaf_peer(a, b):
        return (g, lax.rem(z + a, NZ) * NX + lax.rem(x + b, NX))

    def plane_peer(a, b):
        return (lax.rem(g + a, NG), z * NX + lax.rem(x + b, NX))

    def each(lo, hi, f):
        def step(k, c):
            f(k)
            return c

        lax.fori_loop(lo, hi, step, 0)

    def others(count, f):
        for b in range(1, NX):
            f(0, b)

        def rest(a):
            for b in range(NX):
                f(a, b)

        each(1, count, rest)

    barrier = pltpu.get_barrier_semaphore()

    def hello(peer):
        pl.semaphore_signal(barrier, inc=1, device_id=peer, device_id_type=MESH)

    others(NZ, lambda a, b: hello(leaf_peer(a, b)))
    others(NG, lambda a, b: hello(plane_peer(a, b)))

    loads = [
        pltpu.make_async_copy(a, b, s_in.at[i])
        for i, (a, b) in enumerate(
            [
                (counts_h, counts), (rhs, rhs_s), (basis_h, basis), (owner_h, owner),
                (parent_h, parent), (leaf_h, leaf_t), (mid_h, mid_t), (points, pwin.at[1]),
                (mgeo_h, mgeo), (lgeo_h, lgeo), (ggeo_h, ggeo),
                (partners_h, partners), (peers_h, peers), (slots_h, slots),
                (offsets_h, offsets), (trow_h, trow), (tcol_h, tcol),
            ]
        )
    ]
    for c in loads:
        c.start()

    def copy(src, dst, ss, rs, peer):
        return pltpu.make_async_remote_copy(
            src_ref=src, dst_ref=dst, send_sem=ss, recv_sem=rs, device_id=peer, device_id_type=MESH
        )

    def rs_copy(a, b):
        piece = ptop.at[lax.rem(x + b, NX) * NZ + lax.rem(z + a, NZ)]
        return copy(piece, rsbuf.at[a * NX + b], sends.at[0], recvs.at[0], leaf_peer(a, b))

    def geo_copy(a, b):
        return copy(geo, geos_v.at[d], sends.at[1], recvs.at[1], leaf_peer(a, b))

    def mid_copy(a, b):
        return copy(midc, mids.at[pl.ds(d * 2, 2)], sends.at[2], recvs.at[2], leaf_peer(a, b))

    def tg_copy(k):
        return copy(tgeo, tgeos_v.at[g], sends.at[3], recvs.at[3], (lax.rem(g + k, NG), d))

    def z_copy(k):
        return copy(zbuf.at[z], zbuf.at[z], sends.at[4], recvs.at[4], leaf_peer(k, 0))

    def top_copy(a, b):
        return copy(ztile, tops.at[g * NX + x], sends.at[5], recvs.at[5], plane_peer(a, b))

    whole = [
        rsbuf.at[pl.ds(1, NL - 1)], geos_v.at[pl.ds(0, NL - 1)], mids.at[pl.ds(0, 2 * NL - 2)],
        tgeos_v.at[pl.ds(0, NG - 1)], zbuf.at[pl.ds(0, NZ - 1)], tops.at[pl.ds(0, 31)],
        pwin.at[pl.ds(0, 2)], mwin.at[pl.ds(0, 2)], lwin.at[pl.ds(0, 8)],
    ]

    def got(i):
        pltpu.make_async_copy(whole[i], whole[i], recvs.at[i]).wait()

    def sent(i):
        pltpu.make_async_copy(whole[i], whole[i], sends.at[i]).wait()

    lhalo, phalo = [], []
    for side in range(2):
        part = 2 - 2 * side
        peer = (g, lax.rem(d + (NL - 1 if side == 0 else 1), NL))
        lhalo.append(
            copy(lwin.at[4:8], lwin.at[4 * part : 4 * part + 4], sends.at[8], recvs.at[8], peer)
        )
        phalo.append(copy(pwin.at[1], pwin.at[part], sends.at[6], recvs.at[6], peer))
        phalo.append(copy(mwin.at[1], mwin.at[part], sends.at[7], recvs.at[7], peer))

    lane = lax.broadcasted_iota(jnp.int32, (RHS, PTS), 1)
    for i in range(3):
        loads[i].wait()
    pieces = []
    for l in range(16):
        cols = slice(l * PTS, (l + 1) * PTS)
        m = jnp.where(lane < counts[l], rhs_s[:, cols], 0.0)
        mwin[1, :, cols] = m
        pieces.append(nt(m, basis[l]))
    for i in range(3, 8):
        loads[i].wait()
    srow = lax.broadcasted_iota(jnp.int32, (128, 128), 0) >> 4
    blk = block_of((128, 128))
    total = jnp.zeros((128, RANK), jnp.float32)
    for q in range(4):
        tile = jnp.concatenate(pieces[4 * q : 4 * q + 4], axis=1)
        lwin[4 + q] = tile
        own = jnp.full((128, 128), owner[0, 4 * q], jnp.int32)
        for b in range(1, 4):
            own = jnp.where(blk == b, owner[0, 4 * q + b], own)
        lhs = jnp.where(own == srow, jnp.concatenate([tile] * 8, axis=0), 0.0)
        total = total + nn(lhs, leaf_t[4 * q : 4 * q + 4].reshape(128, RANK))
    srow = lax.broadcasted_iota(jnp.int32, (256, 128), 0) >> 4
    blk = block_of((256, 128))
    topp = jnp.zeros((256, RANK), jnp.float32)
    for q in range(2):
        tile = jnp.concatenate(
            [total[(4 * q + b) * 16 : (4 * q + b + 1) * 16] for b in range(4)], axis=1
        )
        midc[q] = tile
        own = jnp.full((256, 128), parent[0, 4 * q], jnp.int32)
        for b in range(1, 4):
            own = jnp.where(blk == b, parent[0, 4 * q + b], own)
        lhs = jnp.where(own == srow, jnp.concatenate([tile] * 16, axis=0), 0.0)
        topp = topp + nn(lhs, mid_t[4 * q : 4 * q + 4].reshape(128, RANK))
    for q in range(4):
        tile = jnp.concatenate(
            [topp[(4 * q + b) * 16 : (4 * q + b + 1) * 16] for b in range(4)], axis=1
        )
        for i in range(8):
            ptop[q * 8 + i] = tile[2 * i : 2 * i + 2]

    for i in range(8, 17):
        loads[i].wait()
    lane1 = lax.broadcasted_iota(jnp.int32, (1, 128), 1)
    row = jnp.zeros((1, 128), jnp.float32)
    for c in range(4):
        for i in range(8):
            row = jnp.where(lane1 == c * 8 + i, mgeo[c, i], row)
        for i in range(16):
            row = jnp.where(lane1 == 32 + c * 16 + i, lgeo[c, i], row)
    geo[...] = row
    geos_v[d] = row
    row = jnp.zeros((1, 128), jnp.float32)
    for c in range(4):
        for i in range(16):
            row = jnp.where(lane1 == c * 16 + i, ggeo[c, i], row)
    tgeo[...] = row
    tgeos_v[g] = row

    pl.semaphore_wait(barrier, 62)
    others(NZ, lambda a, b: rs_copy(a, b).start())
    for c in phalo:
        c.start()
    others(NZ, lambda a, b: geo_copy(a, b).start())
    each(1, NG, lambda k: tg_copy(k).start())
    for c in lhalo:
        c.start()

    def make_w(l):
        w_s[l] = dot3(leaf_t[l], basis[l], 0, 0)

    loop(16, 4, make_w)

    def window(part, i):
        cols = pl.ds(pl.multiple_of(i * PTS, PTS), PTS)
        m = mwin[part, :, cols]
        high = bf(m)
        w = part * 16 + i
        mhl[w] = jnp.concatenate([high, bf(m - high.astype(jnp.float32))], axis=0)
        c = pwin[part, :, cols] * RATE
        pts[w] = jnp.concatenate([c, jnp.zeros((5, PTS), jnp.float32)], axis=0)

    loop(16, 4, lambda i: window(1, i))

    def distances(l, kb):
        target = pts[l + 16].T
        for c in range(3):
            tb[c] = jnp.broadcast_to(target[:, c : c + 1], (PTS, PTS))
        for j in range(8):
            w = l + 16 + partners[l, j]
            squared = None
            for c in range(3):
                diff = tb[c] - pts[w, c : c + 1, :]
                squared = diff * diff if squared is None else squared + diff * diff
            k = kappa(squared)
            high = bf(k)
            cols = slice((j % 2) * PTS, (j % 2 + 1) * PTS)
            kb[j // 2, 0:PTS, cols] = high
            kb[j // 2, PTS : 2 * PTS, cols] = bf(k - high.astype(jnp.float32))

    def products(l, kb):
        acc = jnp.zeros((2 * RHS, 2 * PTS), jnp.float32)
        for j in range(4):
            ws = [l + 16 + partners[l, 2 * j + e] for e in range(2)]
            m = jnp.concatenate([mhl[w] for w in ws], axis=1)
            acc = acc + raw(m, kb[j], 1, 1)
        base_s[l] = acc[:RHS, :PTS] + (acc[RHS:, :PTS] + acc[:RHS, PTS:])

    def near(i):
        distances(2 * i + 1, kb1)
        products(2 * i, kb0)
        distances(jnp.minimum(2 * i + 2, 15), kb0)
        products(2 * i + 1, kb1)

    got(6)
    got(7)
    loop(16, 4, lambda i: window(0, i))
    loop(16, 4, lambda i: window(2, i))
    distances(0, kb0)
    each(0, N1, near)

    got(0)
    terms = [ptop[x * 8 + z]] + [rsbuf[k] for k in range(1, NL)]
    while len(terms) > 1:
        terms = [a + b for a, b in zip(terms[::2], terms[1::2])]
    zbuf[z] = terms[0]
    each(1, NZ, lambda k: z_copy(k).start())
    others(NZ, lambda a, b: mid_copy(a, b).start())
    mids[pl.ds(d * 2, 2)] = midc[...]
    each(N1, N2, near)
    got(4)
    for i in range(8):
        ztile[2 * i : 2 * i + 2] = zbuf[i]
    others(NG, lambda a, b: top_copy(a, b).start())
    tops[g * NX + x] = ztile[...]
    each(N2, 8, near)

    got(1)
    got(3)
    got(8)
    to_smem = [
        pltpu.make_async_copy(geos_v, geos, s_in.at[0]),
        pltpu.make_async_copy(tgeos_v, tgeos, s_in.at[1]),
    ]
    for c in to_smem:
        c.start()
    for c in to_smem:
        c.wait()

    blk16 = block_of((RHS, 128))
    blk1 = block_of((1, 128))

    def gather(tab, srcs):
        acc = None
        for j, s in enumerate(srcs):
            t = pltpu.roll(tab[s >> 2], ((j - (s & 3)) & 3) * 32, 1)
            acc = t if j == 0 else jnp.where(blk16 == j, t, acc)
        return acc

    def target_nodes(read):
        h = read(3)
        return [(read(c) + h * tcol[c]) * RATE for c in range(3)]

    def coupling(tnodes, reads):
        def mix(c):
            v = jnp.full((1, 128), reads[0](c), jnp.float32)
            for j in range(1, 4):
                v = jnp.where(blk1 == j, reads[j](c), v)
            return v

        h = mix(3)
        squared = None
        for c in range(3):
            r = (mix(c) + h * trow[c : c + 1, :]) * RATE
            diff = tnodes[c] - r
            squared = diff * diff if squared is None else squared + diff * diff
        return kappa(squared)

    def top_read(s):
        return lambda c: tgeos[s >> 4, 0, c * 16 + (s & 15)]

    def mid_read(i):
        return lambda c: geos[i >> 3, 0, c * 8 + (i & 7)]

    def leaf_read(w):
        dev = lax.rem(d + NL - 1 + (w >> 4), NL)
        return lambda c: geos[dev, 0, 32 + c * 16 + (w & 15)]

    def leaf_far(l):
        nodes = target_nodes(leaf_read(l + 16))
        cs, ss = [], []
        for q in range(2):
            srcs = [l + 16 + partners[l, 8 + 4 * q + j] for j in range(4)]
            cs.append(gather(lwin, srcs))
            ss.append(coupling(nodes, [leaf_read(s) for s in srcs]))
        local = nt(jnp.concatenate(cs, axis=1), jnp.concatenate(ss, axis=1))
        base_s[l] += nn(local, basis[l])

    loop(16, 2, leaf_far)

    def top_sources(b):
        p = parent[0, b]
        t = g * 16 + p
        return t, [[(t + offsets[p, 4 * q + j]) & 127 for j in range(4)] for q in range(4)]

    def top_coupling(b):
        t, srcs = top_sources(b)
        nodes = target_nodes(top_read(t))
        s = [coupling(nodes, [top_read(i) for i in four]) for four in srcs]
        p_s[b] = nn(mid_t[b], jnp.concatenate(s, axis=1))

    loop(8, 2, top_coupling)

    got(2)

    def mid_coupling(b):
        nodes = target_nodes(mid_read(d * 8 + b))
        cs, ss = [], []
        for q in range(2):
            srcs = [peers[b, 4 * q + j] * 8 + slots[b, 4 * q + j] for j in range(4)]
            cs.append(gather(mids, srcs))
            ss.append(coupling(nodes, [mid_read(s) for s in srcs]))
        far_m[b] = nt(jnp.concatenate(cs, axis=1), jnp.concatenate(ss, axis=1))

    loop(8, 2, mid_coupling)

    got(5)

    def down_mid(b):
        _, srcs = top_sources(b)
        c = jnp.concatenate([gather(tops, four) for four in srcs], axis=1)
        mid_s[b] = far_m[b] + nt(c, p_s[b])

    loop(8, 4, down_mid)

    for l in range(16):
        cols = slice(l * PTS, (l + 1) * PTS)
        value = base_s[l] + nn(mid_s[owner[0, l]], w_s[l])
        out[:, cols] = value

    for i in range(9):
        sent(i)


N1 = 2
N2 = 4
VM = pl.BlockSpec(memory_space=pltpu.VMEM)
SM = pl.BlockSpec(memory_space=pltpu.SMEM)
ANY = pl.BlockSpec(memory_space=pl.ANY)


def on_device(
    points, rhs, counts, basis, leaf_geom, leaf_partners, leaf_middle_owner, leaf_basis_transfer,
    mid_geom, mid_parent, mid_transfer, mid_peers, mid_slots, top_geom, top_offsets,
):
    table = node_table()
    trow = np.zeros((8, 128), np.float32)
    trow[:3] = np.tile(table, (1, 4))
    tcol = np.broadcast_to(table[:, :, None], (3, 32, 128)).astype(np.float32)
    dma = pltpu.SemaphoreType.DMA

    def vm(*shape, dtype=jnp.float32):
        return pltpu.VMEM(shape, dtype)

    def sm(*shape, dtype=jnp.int32):
        return pltpu.SMEM(shape, dtype)

    product = pl.pallas_call(
        whole_kernel,
        out_shape=jax.ShapeDtypeStruct((16, 2048), jnp.float32),
        in_specs=[ANY] * 17,
        out_specs=VM,
        scratch_shapes=[
            sm(16), sm(1, 16), sm(1, 8), sm(16, 16), sm(8, 8), sm(8, 8), sm(16, 16),
            sm(4, 8, dtype=jnp.float32), sm(4, 16, dtype=jnp.float32),
            sm(4, 16, dtype=jnp.float32), vm(8, 128), vm(3, 32, 128),
            vm(16, 2048), vm(16, 32, 128), vm(16, 32, 32), vm(8, 32, 32),
            vm(3, 16, 2048), vm(3, 3, 2048), vm(12, 16, 128), vm(2, 16, 128), vm(32, 2, 128),
            vm(1, 128), vm(1, 128),
            vm(64, 16, 128), pltpu.SMEM((32, 1, 128), jnp.float32),
            pltpu.SMEM((8, 1, 128), jnp.float32), vm(32, 16, 128),
            vm(32, 2, 128), vm(8, 2, 128), vm(16, 128),
            vm(48, 32, 128, dtype=jnp.bfloat16), vm(48, 8, 128),
            vm(3, 128, 128), vm(4, 256, 256, dtype=jnp.bfloat16),
            vm(4, 256, 256, dtype=jnp.bfloat16),
            vm(16, 16, 128), vm(8, 16, 32), vm(8, 32, 512), vm(16, 32, 128), vm(8, 16, 32),
            vm(32, 1, 128), vm(8, 1, 128),
            dma((17,)), dma((9,)), dma((9,)),
        ],
        compiler_params=pltpu.CompilerParams(collective_id=0, has_side_effects=True),
        name="whole",
    )(
        counts, leaf_middle_owner, mid_parent, leaf_partners, mid_peers, mid_slots, top_offsets,
        mid_geom.T, leaf_geom.T, top_geom.T,
        points, rhs, jnp.swapaxes(basis, 1, 2), leaf_basis_transfer, mid_transfer,
        jnp.asarray(trow), jnp.asarray(tcol),
    )
    return pl.pallas_call(
        mask_kernel,
        out_shape=jax.ShapeDtypeStruct((16, 2048), jnp.float32),
        in_specs=[SM, VM],
        out_specs=VM,
        name="mask",
    )(counts, product)


def solution(mesh):
    both = ("group", "leaf")
    placed = (
        P(None, both), P(None, both), P(both), P(both, None, None), P(both, None), P(both, None),
        P(both, None), P(both, None, None), P(both, None), P("group", "leaf"), P(both, None, None),
        P(both, None), P(both, None), P("group", None), P("group", None),
    )
    return jax.shard_map(
        on_device, mesh=mesh, in_specs=placed, out_specs=P(None, both), check_vma=False
    )
```

time: 53.3 us -> 42.4 us (0.80)
  the two profiles are of different devices: /device:TPU:1 before, /device:TPU:88 now
where the time goes in v3:
time: 42.4 us; the launch traced here: 42.3 us
  Pallas kernels  42.3 us (100%)
    pallas_call x1, Pallas kernels, on_device(): pl.pallas_call(whole_kernel, out_shape=jax.ShapeDtypeStruct((16, 2048), j...  40.7 us
    pallas_call x1, Pallas kernels, on_device(): pl.pallas_call(mask_kernel, out_shape=jax.ShapeDtypeStruct((16, 2048), jn...  1.58 us

profile of v3, /device:TPU:88, one launch (start us, length us, event | category | flops | bytes accessed | tf_op | source)
XLA Modules:
  0.0 42.3 jit_solution(2874081789310808883)
XLA Ops:
  0.0 40.7 %whole.1.product = f32[16,2048]{1,0:T(8,128)} custom-call(s32[16]{0:T(128)} %counts.1, s32[1,16]{1,0:T(1,128)} %owner_h.1, s32[1,8]{1,0:T(1,128)} %parent_h.1, s32[16,16]{1,0:T(8,128)} %partners_h.1, s32[8,8]{1,0:T(8,128)} %peers_h.1, s32[8,8]{1,0:T(8,128)} %slots_h.1, s32[16,16]{1,0:T(8,128)} %offsets_h.1, f32[4,8]{1,0:T(4,128)} %bitcast.5, ...), custom_call_target="tpu_custom_call" | custom-call | tf_op jit(solution)/shard_map/whole/pallas_call | solution.py:455
  40.7 1.6 %mask.1 = f32[16,2048]{1,0:T(8,128)} custom-call(s32[16]{0:T(128)} %counts.1, f32[16,2048]{1,0:T(8,128)} %whole.1.product), custom_call_target="tpu_custom_call" | custom-call | tf_op jit(solution)/shard_map/mask/pallas_call | solution.py:485

commit v4 on v3

--- a/solution.py
+++ b/solution.py
@@ -54,7 +54,7 @@
 def kappa(squared):
     squared = jnp.maximum(squared, 1e-30)
     t = squared * lax.rsqrt(squared)
-    return (1.0 + t) * jnp.exp(-t)
+    return (1.0 + t) * jnp.exp2(t * -1.4426950408889634)
 
 
 def block_of(shape):
@@ -84,7 +84,7 @@
     counts, owner, parent, partners, peers, slots, offsets, mgeo, lgeo, ggeo, trow, tcol,
     rhs_s, basis, leaf_t, mid_t, mwin, pwin, lwin, midc, ptop, geo, tgeo,
     mids, geos, tgeos, tops, rsbuf, zbuf, ztile,
-    mhl, pts, tb, kb0, kb1, base_s, far_m, p_s, w_s, mid_s, geos_v, tgeos_v,
+    mhl, awin, bwin, sb0, sb1, kb0, kb1, base_s, far_l, far_m, p_s, w_s, mid_s, geos_v, tgeos_v,
     s_in, sends, recvs,
 ):
     g = lax.axis_index("group")
@@ -150,8 +150,18 @@
     def geo_copy(a, b):
         return copy(geo, geos_v.at[d], sends.at[1], recvs.at[1], leaf_peer(a, b))
 
-    def mid_copy(a, b):
-        return copy(midc, mids.at[pl.ds(d * 2, 2)], sends.at[2], recvs.at[2], leaf_peer(a, b))
+    def mid_copy(step, k):
+        if step == 0:
+            i = x * NZ + z
+            return copy(midc.at[0], mids.at[i], sends.at[2], recvs.at[2], leaf_peer(k, 0))
+        if step == 1:
+            i = NL + z * NX + x
+            return copy(midc.at[1], mids.at[i], sends.at[9], recvs.at[9], leaf_peer(0, k))
+        if step == 2:
+            block = mids.at[pl.ds(x * NZ, NZ)]
+            return copy(block, block, sends.at[10], recvs.at[10], leaf_peer(0, k))
+        block = mids.at[pl.ds(NL + z * NX, NX)]
+        return copy(block, block, sends.at[11], recvs.at[11], leaf_peer(k, 0))
 
     def tg_copy(k):
         return copy(tgeo, tgeos_v.at[g], sends.at[3], recvs.at[3], (lax.rem(g + k, NG), d))
@@ -163,9 +173,11 @@
         return copy(ztile, tops.at[g * NX + x], sends.at[5], recvs.at[5], plane_peer(a, b))
 
     whole = [
-        rsbuf.at[pl.ds(1, NL - 1)], geos_v.at[pl.ds(0, NL - 1)], mids.at[pl.ds(0, 2 * NL - 2)],
+        rsbuf.at[pl.ds(1, NL - 1)], geos_v.at[pl.ds(0, NL - 1)], mids.at[pl.ds(0, NZ - 1)],
         tgeos_v.at[pl.ds(0, NG - 1)], zbuf.at[pl.ds(0, NZ - 1)], tops.at[pl.ds(0, 31)],
         pwin.at[pl.ds(0, 2)], mwin.at[pl.ds(0, 2)], lwin.at[pl.ds(0, 8)],
+        mids.at[pl.ds(0, NX - 1)], mids.at[pl.ds(0, NZ * (NX - 1))],
+        mids.at[pl.ds(0, NX * (NZ - 1))],
     ]
 
     def got(i):
@@ -244,6 +256,38 @@
     tgeo[...] = row
     tgeos_v[g] = row
 
+    def make_w(l):
+        w_s[l] = dot3(leaf_t[l], basis[l], 0, 0)
+
+    loop(16, 4, make_w)
+
+    sub = lax.broadcasted_iota(jnp.int32, (8, PTS), 0)
+
+    def split3(v):
+        a = bf(v).astype(jnp.float32)
+        r = v - a
+        b = bf(r).astype(jnp.float32)
+        return a, b, r - b
+
+    def window(part, i):
+        cols = pl.ds(pl.multiple_of(i * PTS, PTS), PTS)
+        m = mwin[part, :, cols]
+        high = bf(m)
+        w = part * 16 + i
+        mhl[w] = jnp.concatenate([high, bf(m - high.astype(jnp.float32))], axis=0)
+        c = (pwin[part, :, cols] - 0.5) * RATE
+        norm = jnp.sum(c * c, axis=0, keepdims=True)
+        c8 = jnp.concatenate([c, jnp.zeros((5, PTS), jnp.float32)], axis=0)
+        v = jnp.where(sub == 3, norm, jnp.where(sub == 4, 1.0, c8))
+        a, b, e = split3(v)
+        bwin[w] = bf(jnp.concatenate([a, a, a, b, b, e], axis=0))
+        if part == 1:
+            v = jnp.where(sub == 3, 1.0, jnp.where(sub == 4, norm, -2.0 * c8))
+            a, b, e = split3(v)
+            awin[i] = bf(jnp.concatenate([a, b, e, a, b, a], axis=0).T)
+
+    loop(16, 4, lambda i: window(1, i))
+
     pl.semaphore_wait(barrier, 62)
     others(NZ, lambda a, b: rs_copy(a, b).start())
     for c in phalo:
@@ -252,38 +296,23 @@
     each(1, NG, lambda k: tg_copy(k).start())
     for c in lhalo:
         c.start()
-
-    def make_w(l):
-        w_s[l] = dot3(leaf_t[l], basis[l], 0, 0)
-
-    loop(16, 4, make_w)
-
-    def window(part, i):
-        cols = pl.ds(pl.multiple_of(i * PTS, PTS), PTS)
-        m = mwin[part, :, cols]
-        high = bf(m)
-        w = part * 16 + i
-        mhl[w] = jnp.concatenate([high, bf(m - high.astype(jnp.float32))], axis=0)
-        c = pwin[part, :, cols] * RATE
-        pts[w] = jnp.concatenate([c, jnp.zeros((5, PTS), jnp.float32)], axis=0)
-
-    loop(16, 4, lambda i: window(1, i))
-
-    def distances(l, kb):
-        target = pts[l + 16].T
-        for c in range(3):
-            tb[c] = jnp.broadcast_to(target[:, c : c + 1], (PTS, PTS))
-        for j in range(8):
-            w = l + 16 + partners[l, j]
-            squared = None
-            for c in range(3):
-                diff = tb[c] - pts[w, c : c + 1, :]
-                squared = diff * diff if squared is None else squared + diff * diff
-            k = kappa(squared)
+    each(1, NZ, lambda k: mid_copy(0, k).start())
+    for k in range(1, NX):
+        mid_copy(1, k).start()
+    mids[x * NZ + z] = midc[0]
+    mids[NL + z * NX + x] = midc[1]
+
+    def distances(l, sb):
+        for j in range(4):
+            ws = [l + 16 + partners[l, 2 * j + e] for e in range(2)]
+            sb[j] = raw(awin[l], jnp.concatenate([bwin[w] for w in ws], axis=1), 1, 0)
+
+    def kernels(sb, kb):
+        for j in range(4):
+            k = kappa(sb[j])
             high = bf(k)
-            cols = slice((j % 2) * PTS, (j % 2 + 1) * PTS)
-            kb[j // 2, 0:PTS, cols] = high
-            kb[j // 2, PTS : 2 * PTS, cols] = bf(k - high.astype(jnp.float32))
+            kb[j, 0:PTS] = high
+            kb[j, PTS : 2 * PTS] = bf(k - high.astype(jnp.float32))
 
     def products(l, kb):
         acc = jnp.zeros((2 * RHS, 2 * PTS), jnp.float32)
@@ -294,45 +323,12 @@
         base_s[l] = acc[:RHS, :PTS] + (acc[RHS:, :PTS] + acc[:RHS, PTS:])
 
     def near(i):
-        distances(2 * i + 1, kb1)
+        distances(jnp.minimum(2 * i + 2, 15), sb0)
+        kernels(sb1, kb1)
         products(2 * i, kb0)
-        distances(jnp.minimum(2 * i + 2, 15), kb0)
+        distances(jnp.minimum(2 * i + 3, 15), sb1)
+        kernels(sb0, kb0)
         products(2 * i + 1, kb1)
-
-    got(6)
-    got(7)
-    loop(16, 4, lambda i: window(0, i))
-    loop(16, 4, lambda i: window(2, i))
-    distances(0, kb0)
-    each(0, N1, near)
-
-    got(0)
-    terms = [ptop[x * 8 + z]] + [rsbuf[k] for k in range(1, NL)]
-    while len(terms) > 1:
-        terms = [a + b for a, b in zip(terms[::2], terms[1::2])]
-    zbuf[z] = terms[0]
-    each(1, NZ, lambda k: z_copy(k).start())
-    others(NZ, lambda a, b: mid_copy(a, b).start())
-    mids[pl.ds(d * 2, 2)] = midc[...]
-    each(N1, N2, near)
-    got(4)
-    for i in range(8):
-        ztile[2 * i : 2 * i + 2] = zbuf[i]
-    others(NG, lambda a, b: top_copy(a, b).start())
-    tops[g * NX + x] = ztile[...]
-    each(N2, 8, near)
-
-    got(1)
-    got(3)
-    got(8)
-    to_smem = [
-        pltpu.make_async_copy(geos_v, geos, s_in.at[0]),
-        pltpu.make_async_copy(tgeos_v, tgeos, s_in.at[1]),
-    ]
-    for c in to_smem:
-        c.start()
-    for c in to_smem:
-        c.wait()
 
     blk16 = block_of((RHS, 128))
     blk1 = block_of((1, 128))
@@ -372,6 +368,56 @@
     def leaf_read(w):
         dev = lax.rem(d + NL - 1 + (w >> 4), NL)
         return lambda c: geos[dev, 0, 32 + c * 16 + (w & 15)]
+
+    got(3)
+    to_smem = pltpu.make_async_copy(tgeos_v, tgeos, s_in.at[1])
+    to_smem.start()
+    to_smem.wait()
+
+    def top_sources(b):
+        p = parent[0, b]
+        t = g * 16 + p
+        return t, [[(t + offsets[p, 4 * q + j]) & 127 for j in range(4)] for q in range(4)]
+
+    def top_coupling(b):
+        t, srcs = top_sources(b)
+        nodes = target_nodes(top_read(t))
+        s = [coupling(nodes, [top_read(i) for i in four]) for four in srcs]
+        p_s[b] = nn(mid_t[b], jnp.concatenate(s, axis=1))
+
+    loop(8, 4, top_coupling)
+
+    got(0)
+    terms = [ptop[x * 8 + z]] + [rsbuf[k] for k in range(1, NL)]
+    while len(terms) > 1:
+        terms = [a + b for a, b in zip(terms[::2], terms[1::2])]
+    zbuf[z] = terms[0]
+    each(1, NZ, lambda k: z_copy(k).start())
+    got(2)
+    got(9)
+    for k in range(1, NX):
+        mid_copy(2, k).start()
+    each(1, NZ, lambda k: mid_copy(3, k).start())
+    got(6)
+    got(7)
+    loop(16, 4, lambda i: window(0, i))
+    loop(16, 4, lambda i: window(2, i))
+    distances(0, sb0)
+    kernels(sb0, kb0)
+    distances(1, sb1)
+    each(0, N2, near)
+    got(4)
+    for i in range(8):
+        ztile[2 * i : 2 * i + 2] = zbuf[i]
+    others(NG, lambda a, b: top_copy(a, b).start())
+    tops[g * NX + x] = ztile[...]
+    each(N2, 8, near)
+
+    got(1)
+    got(8)
+    to_smem = pltpu.make_async_copy(geos_v, geos, s_in.at[0])
+    to_smem.start()
+    to_smem.wait()
 
     def leaf_far(l):
         nodes = target_nodes(leaf_read(l + 16))
@@ -381,35 +427,27 @@
             cs.append(gather(lwin, srcs))
             ss.append(coupling(nodes, [leaf_read(s) for s in srcs]))
         local = nt(jnp.concatenate(cs, axis=1), jnp.concatenate(ss, axis=1))
-        base_s[l] += nn(local, basis[l])
-
-    loop(16, 2, leaf_far)
-
-    def top_sources(b):
-        p = parent[0, b]
-        t = g * 16 + p
-        return t, [[(t + offsets[p, 4 * q + j]) & 127 for j in range(4)] for q in range(4)]
-
-    def top_coupling(b):
-        t, srcs = top_sources(b)
-        nodes = target_nodes(top_read(t))
-        s = [coupling(nodes, [top_read(i) for i in four]) for four in srcs]
-        p_s[b] = nn(mid_t[b], jnp.concatenate(s, axis=1))
-
-    loop(8, 2, top_coupling)
-
-    got(2)
+        far_l[l] = nn(local, basis[l])
+
+    loop(16, 4, leaf_far)
+
+    got(10)
+    got(11)
 
     def mid_coupling(b):
         nodes = target_nodes(mid_read(d * 8 + b))
         cs, ss = [], []
         for q in range(2):
-            srcs = [peers[b, 4 * q + j] * 8 + slots[b, 4 * q + j] for j in range(4)]
-            cs.append(gather(mids, srcs))
+            named = [(peers[b, 4 * q + j], slots[b, 4 * q + j]) for j in range(4)]
+            srcs = [p * 8 + i for p, i in named]
+            places = [
+                jnp.where(i < 4, (p & 3) * NZ + (p >> 2), NL + p) * 4 + (i & 3) for p, i in named
+            ]
+            cs.append(gather(mids, places))
             ss.append(coupling(nodes, [mid_read(s) for s in srcs]))
         far_m[b] = nt(jnp.concatenate(cs, axis=1), jnp.concatenate(ss, axis=1))
 
-    loop(8, 2, mid_coupling)
+    loop(8, 4, mid_coupling)
 
     got(5)
 
@@ -422,14 +460,13 @@
 
     for l in range(16):
         cols = slice(l * PTS, (l + 1) * PTS)
-        value = base_s[l] + nn(mid_s[owner[0, l]], w_s[l])
+        value = base_s[l] + far_l[l] + nn(mid_s[owner[0, l]], w_s[l])
         out[:, cols] = value
 
-    for i in range(9):
+    for i in range(12):
         sent(i)
 
 
-N1 = 2
 N2 = 4
 VM = pl.BlockSpec(memory_space=pltpu.VMEM)
 SM = pl.BlockSpec(memory_space=pltpu.SMEM)
@@ -454,7 +491,7 @@
 
     product = pl.pallas_call(
         whole_kernel,
-        out_shape=jax.ShapeDtypeStruct((16, 2048), jnp.float32),
+        out_shape=pltpu.VMEM((16, 2048), jnp.float32),
         in_specs=[ANY] * 17,
         out_specs=VM,
         scratch_shapes=[
@@ -467,12 +504,13 @@
             vm(64, 16, 128), pltpu.SMEM((32, 1, 128), jnp.float32),
             pltpu.SMEM((8, 1, 128), jnp.float32), vm(32, 16, 128),
             vm(32, 2, 128), vm(8, 2, 128), vm(16, 128),
-            vm(48, 32, 128, dtype=jnp.bfloat16), vm(48, 8, 128),
-            vm(3, 128, 128), vm(4, 256, 256, dtype=jnp.bfloat16),
+            vm(48, 32, 128, dtype=jnp.bfloat16), vm(16, 128, 48, dtype=jnp.bfloat16),
+            vm(48, 48, 128, dtype=jnp.bfloat16), vm(4, 128, 256), vm(4, 128, 256),
             vm(4, 256, 256, dtype=jnp.bfloat16),
-            vm(16, 16, 128), vm(8, 16, 32), vm(8, 32, 512), vm(16, 32, 128), vm(8, 16, 32),
+            vm(4, 256, 256, dtype=jnp.bfloat16),
+            vm(16, 16, 128), vm(16, 16, 128), vm(8, 16, 32), vm(8, 32, 512), vm(16, 32, 128), vm(8, 16, 32),
             vm(32, 1, 128), vm(8, 1, 128),
-            dma((17,)), dma((9,)), dma((9,)),
+            dma((17,)), dma((12,)), dma((12,)),
         ],
         compiler_params=pltpu.CompilerParams(collective_id=0, has_side_effects=True),
         name="whole",
@@ -488,7 +526,7 @@
         in_specs=[SM, VM],
         out_specs=VM,
         name="mask",
-    )(counts, product)
+    )(counts, pltpu.with_memory_space_constraint(product, pltpu.VMEM))
 
 
 def solution(mesh):

time: 42.4 us -> 34.5 us (0.81)
  the two profiles are of different devices: /device:TPU:88 before, /device:TPU:32 now
where the time goes in v4:
time: 34.5 us; the launch traced here: 34.4 us
  Pallas kernels  34.4 us (100%)
    pallas_call x1, Pallas kernels, on_device(): pl.pallas_call(whole_kernel, out_shape=pltpu.VMEM((16, 2048), jnp.float32...  33 us
    pallas_call x1, Pallas kernels, on_device(): pl.pallas_call(mask_kernel, out_shape=jax.ShapeDtypeStruct((16, 2048), jn...  1.33 us

profile of v4, /device:TPU:32, one launch (start us, length us, event | category | flops | bytes accessed | tf_op | source)
XLA Modules:
  0.0 34.4 jit_solution(600523685546559709)
XLA Ops:
  0.0 33.0 %whole.1.product = f32[16,2048]{1,0:T(8,128)S(1)} custom-call(s32[16]{0:T(128)} %counts.1, s32[1,16]{1,0:T(1,128)} %owner_h.1, s32[1,8]{1,0:T(1,128)} %parent_h.1, s32[16,16]{1,0:T(8,128)} %partners_h.1, s32[8,8]{1,0:T(8,128)} %peers_h.1, s32[8,8]{1,0:T(8,128)} %slots_h.1, s32[16,16]{1,0:T(8,128)} %offsets_h.1, f32[4,8]{1,0:T(4,128)} %bitcast.5, ...), custom_call_target="tpu_custom_call" | custom-call | tf_op jit(solution)/shard_map/whole/pallas_call | solution.py:492
  33.1 1.3 %mask.1 = f32[16,2048]{1,0:T(8,128)} custom-call(s32[16]{0:T(128)} %counts.1, f32[16,2048]{1,0:T(8,128)S(1)} %whole.1.product), custom_call_target="tpu_custom_call" | custom-call | tf_op jit(solution)/shard_map/mask/pallas_call | solution.py:523

commit v5 on v4

--- a/solution.py
+++ b/solution.py
@@ -70,11 +70,15 @@
     lax.fori_loop(0, count // width, step, 0)
 
 
-def mask_kernel(counts, product, out):
-    lane = lax.broadcasted_iota(jnp.int32, (RHS, PTS), 1)
-    for l in range(16):
-        cols = slice(l * PTS, (l + 1) * PTS)
-        out[:, cols] = jnp.where(lane < counts[l], product[:, cols], 0.0)
+def store_kernel(product, out, sems):
+    parts = [
+        pltpu.make_async_copy(product.at[8 * i : 8 * i + 8], out.at[8 * i : 8 * i + 8], sems.at[i])
+        for i in range(2)
+    ]
+    for c in parts:
+        c.start()
+    for c in parts:
+        c.wait()
 
 
 def whole_kernel(
@@ -83,8 +87,8 @@
     out,
     counts, owner, parent, partners, peers, slots, offsets, mgeo, lgeo, ggeo, trow, tcol,
     rhs_s, basis, leaf_t, mid_t, mwin, pwin, lwin, midc, ptop, geo, tgeo,
-    mids, geos, tgeos, tops, rsbuf, zbuf, ztile,
-    mhl, awin, bwin, sb0, sb1, kb0, kb1, base_s, far_l, far_m, p_s, w_s, mid_s, geos_v, tgeos_v,
+    mids, geos, tgeos, lgeos, tops, rsbuf, zbuf, ztile,
+    mhl, awin, bwin, sb0, sb1, kb0, kb1, base_s, far_l, far_m, p_s, w_s, mid_s, geos_v, tgeos_v, lgeos_v,
     s_in, sends, recvs,
 ):
     g = lax.axis_index("group")
@@ -92,11 +96,18 @@
     z = d // NX
     x = d % NX
 
+    y = g // 2
+    core = g % 2
+    xs = [x] + [lax.rem(x + b, NX) for b in range(1, NX)]
+    zs = [z] + [lax.rem(z + a, NZ) for a in range(1, NZ)]
+    ys = [y] + [lax.rem(y + a, 4) for a in range(1, 4)]
+    cs = [core, 1 - core]
+
     def leaf_peer(a, b):
-        return (g, lax.rem(z + a, NZ) * NX + lax.rem(x + b, NX))
+        return (g, zs[a] * NX + xs[b])
 
     def plane_peer(a, b):
-        return (lax.rem(g + a, NG), z * NX + lax.rem(x + b, NX))
+        return (ys[a // 2] * 2 + cs[a % 2], z * NX + xs[b])
 
     def each(lo, hi, f):
         def step(k, c):
@@ -106,14 +117,13 @@
         lax.fori_loop(lo, hi, step, 0)
 
     def others(count, f):
-        for b in range(1, NX):
-            f(0, b)
-
-        def rest(a):
-            for b in range(NX):
-                f(a, b)
-
-        each(1, count, rest)
+        def hops(a, b):
+            along = min(a, NZ - a) if count == NZ else min(a // 2, 4 - a // 2)
+            return along + min(b, NX - b)
+
+        pairs = [(a, b) for a in range(8) for b in range(NX) if (a, b) != (0, 0)]
+        for a, b in sorted(pairs, key=lambda p: -hops(*p)):
+            f(a, b)
 
     barrier = pltpu.get_barrier_semaphore()
 
@@ -121,7 +131,7 @@
         pl.semaphore_signal(barrier, inc=1, device_id=peer, device_id_type=MESH)
 
     others(NZ, lambda a, b: hello(leaf_peer(a, b)))
-    others(NG, lambda a, b: hello(plane_peer(a, b)))
+    others(-1, lambda a, b: hello(plane_peer(a, b)))
 
     loads = [
         pltpu.make_async_copy(a, b, s_in.at[i])
@@ -144,7 +154,7 @@
         )
 
     def rs_copy(a, b):
-        piece = ptop.at[lax.rem(x + b, NX) * NZ + lax.rem(z + a, NZ)]
+        piece = ptop.at[xs[b] * NZ + zs[a]]
         return copy(piece, rsbuf.at[a * NX + b], sends.at[0], recvs.at[0], leaf_peer(a, b))
 
     def geo_copy(a, b):
@@ -169,6 +179,10 @@
     def z_copy(k):
         return copy(zbuf.at[z], zbuf.at[z], sends.at[4], recvs.at[4], leaf_peer(k, 0))
 
+    def ring(f):
+        for k in (4, 3, 5, 2, 6, 1, 7):
+            f(k)
+
     def top_copy(a, b):
         return copy(ztile, tops.at[g * NX + x], sends.at[5], recvs.at[5], plane_peer(a, b))
 
@@ -177,7 +191,7 @@
         tgeos_v.at[pl.ds(0, NG - 1)], zbuf.at[pl.ds(0, NZ - 1)], tops.at[pl.ds(0, 31)],
         pwin.at[pl.ds(0, 2)], mwin.at[pl.ds(0, 2)], lwin.at[pl.ds(0, 8)],
         mids.at[pl.ds(0, NX - 1)], mids.at[pl.ds(0, NZ * (NX - 1))],
-        mids.at[pl.ds(0, NX * (NZ - 1))],
+        mids.at[pl.ds(0, NX * (NZ - 1))], lgeos_v.at[pl.ds(0, 2)],
     ]
 
     def got(i):
@@ -193,6 +207,7 @@
         lhalo.append(
             copy(lwin.at[4:8], lwin.at[4 * part : 4 * part + 4], sends.at[8], recvs.at[8], peer)
         )
+        lhalo.append(copy(geo, lgeos_v.at[part], sends.at[12], recvs.at[12], peer))
         phalo.append(copy(pwin.at[1], pwin.at[part], sends.at[6], recvs.at[6], peer))
         phalo.append(copy(mwin.at[1], mwin.at[part], sends.at[7], recvs.at[7], peer))
 
@@ -249,6 +264,7 @@
             row = jnp.where(lane1 == 32 + c * 16 + i, lgeo[c, i], row)
     geo[...] = row
     geos_v[d] = row
+    lgeos_v[1] = row
     row = jnp.zeros((1, 128), jnp.float32)
     for c in range(4):
         for i in range(16):
@@ -290,13 +306,13 @@
 
     pl.semaphore_wait(barrier, 62)
     others(NZ, lambda a, b: rs_copy(a, b).start())
+    each(1, NG, lambda k: tg_copy(k).start())
+    for c in lhalo:
+        c.start()
     for c in phalo:
         c.start()
     others(NZ, lambda a, b: geo_copy(a, b).start())
-    each(1, NG, lambda k: tg_copy(k).start())
-    for c in lhalo:
-        c.start()
-    each(1, NZ, lambda k: mid_copy(0, k).start())
+    ring(lambda k: mid_copy(0, k).start())
     for k in range(1, NX):
         mid_copy(1, k).start()
     mids[x * NZ + z] = midc[0]
@@ -366,8 +382,7 @@
         return lambda c: geos[i >> 3, 0, c * 8 + (i & 7)]
 
     def leaf_read(w):
-        dev = lax.rem(d + NL - 1 + (w >> 4), NL)
-        return lambda c: geos[dev, 0, 32 + c * 16 + (w & 15)]
+        return lambda c: lgeos[w >> 4, 0, 32 + c * 16 + (w & 15)]
 
     got(3)
     to_smem = pltpu.make_async_copy(tgeos_v, tgeos, s_in.at[1])
@@ -387,17 +402,38 @@
 
     loop(8, 4, top_coupling)
 
+    got(8)
+    got(12)
+    to_smem = pltpu.make_async_copy(lgeos_v, lgeos, s_in.at[0])
+    to_smem.start()
+    to_smem.wait()
+    def leaf_far(l):
+        nodes = target_nodes(leaf_read(l + 16))
+        cs, ss = [], []
+        for q in range(2):
+            srcs = [l + 16 + partners[l, 8 + 4 * q + j] for j in range(4)]
+            cs.append(gather(lwin, srcs))
+            ss.append(coupling(nodes, [leaf_read(s) for s in srcs]))
+        local = nt(jnp.concatenate(cs, axis=1), jnp.concatenate(ss, axis=1))
+        far_l[l] = nn(local, basis[l])
+
+    def leaf_four(q):
+        for e in range(4):
+            leaf_far(4 * q + e)
+
+    each(0, 1, leaf_four)
     got(0)
     terms = [ptop[x * 8 + z]] + [rsbuf[k] for k in range(1, NL)]
     while len(terms) > 1:
         terms = [a + b for a, b in zip(terms[::2], terms[1::2])]
     zbuf[z] = terms[0]
-    each(1, NZ, lambda k: z_copy(k).start())
+    ring(lambda k: z_copy(k).start())
     got(2)
     got(9)
     for k in range(1, NX):
         mid_copy(2, k).start()
-    each(1, NZ, lambda k: mid_copy(3, k).start())
+    ring(lambda k: mid_copy(3, k).start())
+    each(1, 4, leaf_four)
     got(6)
     got(7)
     loop(16, 4, lambda i: window(0, i))
@@ -409,27 +445,14 @@
     got(4)
     for i in range(8):
         ztile[2 * i : 2 * i + 2] = zbuf[i]
-    others(NG, lambda a, b: top_copy(a, b).start())
+    others(-1, lambda a, b: top_copy(a, b).start())
     tops[g * NX + x] = ztile[...]
     each(N2, 8, near)
 
     got(1)
-    got(8)
     to_smem = pltpu.make_async_copy(geos_v, geos, s_in.at[0])
     to_smem.start()
     to_smem.wait()
-
-    def leaf_far(l):
-        nodes = target_nodes(leaf_read(l + 16))
-        cs, ss = [], []
-        for q in range(2):
-            srcs = [l + 16 + partners[l, 8 + 4 * q + j] for j in range(4)]
-            cs.append(gather(lwin, srcs))
-            ss.append(coupling(nodes, [leaf_read(s) for s in srcs]))
-        local = nt(jnp.concatenate(cs, axis=1), jnp.concatenate(ss, axis=1))
-        far_l[l] = nn(local, basis[l])
-
-    loop(16, 4, leaf_far)
 
     got(10)
     got(11)
@@ -461,15 +484,14 @@
     for l in range(16):
         cols = slice(l * PTS, (l + 1) * PTS)
         value = base_s[l] + far_l[l] + nn(mid_s[owner[0, l]], w_s[l])
-        out[:, cols] = value
-
-    for i in range(12):
+        out[:, cols] = jnp.where(lane < counts[l], value, 0.0)
+
+    for i in range(13):
         sent(i)
 
 
-N2 = 4
+N2 = 1
 VM = pl.BlockSpec(memory_space=pltpu.VMEM)
-SM = pl.BlockSpec(memory_space=pltpu.SMEM)
 ANY = pl.BlockSpec(memory_space=pl.ANY)
 
 
@@ -502,15 +524,16 @@
             vm(3, 16, 2048), vm(3, 3, 2048), vm(12, 16, 128), vm(2, 16, 128), vm(32, 2, 128),
             vm(1, 128), vm(1, 128),
             vm(64, 16, 128), pltpu.SMEM((32, 1, 128), jnp.float32),
-            pltpu.SMEM((8, 1, 128), jnp.float32), vm(32, 16, 128),
+            pltpu.SMEM((8, 1, 128), jnp.float32),
+            pltpu.SMEM((3, 1, 128), jnp.float32), vm(32, 16, 128),
             vm(32, 2, 128), vm(8, 2, 128), vm(16, 128),
             vm(48, 32, 128, dtype=jnp.bfloat16), vm(16, 128, 48, dtype=jnp.bfloat16),
             vm(48, 48, 128, dtype=jnp.bfloat16), vm(4, 128, 256), vm(4, 128, 256),
             vm(4, 256, 256, dtype=jnp.bfloat16),
             vm(4, 256, 256, dtype=jnp.bfloat16),
             vm(16, 16, 128), vm(16, 16, 128), vm(8, 16, 32), vm(8, 32, 512), vm(16, 32, 128), vm(8, 16, 32),
-            vm(32, 1, 128), vm(8, 1, 128),
-            dma((17,)), dma((12,)), dma((12,)),
+            vm(32, 1, 128), vm(8, 1, 128), vm(3, 1, 128),
+            dma((17,)), dma((13,)), dma((13,)),
         ],
         compiler_params=pltpu.CompilerParams(collective_id=0, has_side_effects=True),
         name="whole",
@@ -521,12 +544,13 @@
         jnp.asarray(trow), jnp.asarray(tcol),
     )
     return pl.pallas_call(
-        mask_kernel,
+        store_kernel,
         out_shape=jax.ShapeDtypeStruct((16, 2048), jnp.float32),
-        in_specs=[SM, VM],
-        out_specs=VM,
-        name="mask",
-    )(counts, pltpu.with_memory_space_constraint(product, pltpu.VMEM))
+        in_specs=[VM],
+        out_specs=ANY,
+        scratch_shapes=[dma((2,))],
+        name="store",
+    )(pltpu.with_memory_space_constraint(product, pltpu.VMEM))
 
 
 def solution(mesh):

time: 34.5 us -> 32.9 us (0.954)
  the two profiles are of different devices: /device:TPU:32 before, /device:TPU:1 now
where the time goes in v5:
time: 32.9 us; the launch traced here: 32.8 us
  Pallas kernels  32.8 us (100%)
    pallas_call x1, Pallas kernels, on_device(): pl.pallas_call(whole_kernel, out_shape=pltpu.VMEM((16, 2048), jnp.float32...  32.1 us
    pallas_call x1, Pallas kernels, on_device(): pl.pallas_call(store_kernel, out_shape=jax.ShapeDtypeStruct((16, 2048), j...  0.67 us

profile of v5, /device:TPU:1, one launch (start us, length us, event | category | flops | bytes accessed | tf_op | source)
XLA Modules:
  0.0 32.8 jit_solution(7609025571487198194)
XLA Ops:
  0.0 32.1 %whole.1.product = f32[16,2048]{1,0:T(8,128)S(1)} custom-call(s32[16]{0:T(128)} %counts_h.1, s32[1,16]{1,0:T(1,128)} %owner_h.1, s32[1,8]{1,0:T(1,128)} %parent_h.1, s32[16,16]{1,0:T(8,128)} %partners_h.1, s32[8,8]{1,0:T(8,128)} %peers_h.1, s32[8,8]{1,0:T(8,128)} %slots_h.1, s32[16,16]{1,0:T(8,128)} %offsets_h.1, f32[4,8]{1,0:T(4,128)} %bitcast.5, ...), custom_call_target="tpu_custom_call" | custom-call | tf_op jit(solution)/shard_map/whole/pallas_call | solution.py:514
  32.1 0.7 %store.1 = f32[16,2048]{1,0:T(8,128)} custom-call(f32[16,2048]{1,0:T(8,128)S(1)} %whole.1.product), custom_call_target="tpu_custom_call" | custom-call | tf_op jit(solution)/shard_map/store/pallas_call | solution.py:546

commit v6 on v5

--- a/solution.py
+++ b/solution.py
@@ -43,6 +43,16 @@
     return raw(ah, bh, ca, cb) + (raw(al, bh, ca, cb) + raw(ah, bl, ca, cb))
 
 
+def split(a):
+    high = bf(a)
+    return high, bf(a - high.astype(jnp.float32))
+
+
+def dot3_split(a, bh, bl, ca, cb):
+    ah, al = split(a)
+    return raw(ah, bh, ca, cb) + (raw(al, bh, ca, cb) + raw(ah, bl, ca, cb))
+
+
 def nt(a, b):
     return dot3(a, b, 1, 1)
 
@@ -88,7 +98,7 @@
     counts, owner, parent, partners, peers, slots, offsets, mgeo, lgeo, ggeo, trow, tcol,
     rhs_s, basis, leaf_t, mid_t, mwin, pwin, lwin, midc, ptop, geo, tgeo,
     mids, geos, tgeos, lgeos, tops, rsbuf, zbuf, ztile,
-    mhl, awin, bwin, sb0, sb1, kb0, kb1, base_s, far_l, far_m, p_s, w_s, mid_s, geos_v, tgeos_v, lgeos_v,
+    mhl, awin, bwin, sb0, sb1, kb0, kb1, base_s, far_l, far_m, p_h, p_l, w_h, w_l, mid_s, geos_v, tgeos_v, lgeos_v,
     s_in, sends, recvs,
 ):
     g = lax.axis_index("group")
@@ -272,11 +282,6 @@
     tgeo[...] = row
     tgeos_v[g] = row
 
-    def make_w(l):
-        w_s[l] = dot3(leaf_t[l], basis[l], 0, 0)
-
-    loop(16, 4, make_w)
-
     sub = lax.broadcasted_iota(jnp.int32, (8, PTS), 0)
 
     def split3(v):
@@ -327,15 +332,12 @@
         for j in range(4):
             k = kappa(sb[j])
             high = bf(k)
-            kb[j, 0:PTS] = high
-            kb[j, PTS : 2 * PTS] = bf(k - high.astype(jnp.float32))
+            kb[0:PTS, 2 * PTS * j : 2 * PTS * (j + 1)] = high
+            kb[PTS : 2 * PTS, 2 * PTS * j : 2 * PTS * (j + 1)] = bf(k - high.astype(jnp.float32))
 
     def products(l, kb):
-        acc = jnp.zeros((2 * RHS, 2 * PTS), jnp.float32)
-        for j in range(4):
-            ws = [l + 16 + partners[l, 2 * j + e] for e in range(2)]
-            m = jnp.concatenate([mhl[w] for w in ws], axis=1)
-            acc = acc + raw(m, kb[j], 1, 1)
+        m = jnp.concatenate([mhl[l + 16 + partners[l, j]] for j in range(8)], axis=1)
+        acc = raw(m, kb[...], 1, 1)
         base_s[l] = acc[:RHS, :PTS] + (acc[RHS:, :PTS] + acc[:RHS, PTS:])
 
     def near(i):
@@ -384,6 +386,11 @@
     def leaf_read(w):
         return lambda c: lgeos[w >> 4, 0, 32 + c * 16 + (w & 15)]
 
+    def make_w(l):
+        w_h[l], w_l[l] = split(dot3(leaf_t[l], basis[l], 0, 0))
+
+    loop(16, 4, make_w)
+
     got(3)
     to_smem = pltpu.make_async_copy(tgeos_v, tgeos, s_in.at[1])
     to_smem.start()
@@ -398,7 +405,7 @@
         t, srcs = top_sources(b)
         nodes = target_nodes(top_read(t))
         s = [coupling(nodes, [top_read(i) for i in four]) for four in srcs]
-        p_s[b] = nn(mid_t[b], jnp.concatenate(s, axis=1))
+        p_h[b], p_l[b] = split(nn(mid_t[b], jnp.concatenate(s, axis=1)))
 
     loop(8, 4, top_coupling)
 
@@ -477,13 +484,13 @@
     def down_mid(b):
         _, srcs = top_sources(b)
         c = jnp.concatenate([gather(tops, four) for four in srcs], axis=1)
-        mid_s[b] = far_m[b] + nt(c, p_s[b])
-
-    loop(8, 4, down_mid)
+        mid_s[b] = far_m[b] + dot3_split(c, p_h[b], p_l[b], 1, 1)
+
+    loop(8, 8, down_mid)
 
     for l in range(16):
         cols = slice(l * PTS, (l + 1) * PTS)
-        value = base_s[l] + far_l[l] + nn(mid_s[owner[0, l]], w_s[l])
+        value = base_s[l] + far_l[l] + dot3_split(mid_s[owner[0, l]], w_h[l], w_l[l], 1, 0)
         out[:, cols] = jnp.where(lane < counts[l], value, 0.0)
 
     for i in range(13):
@@ -529,9 +536,11 @@
             vm(32, 2, 128), vm(8, 2, 128), vm(16, 128),
             vm(48, 32, 128, dtype=jnp.bfloat16), vm(16, 128, 48, dtype=jnp.bfloat16),
             vm(48, 48, 128, dtype=jnp.bfloat16), vm(4, 128, 256), vm(4, 128, 256),
-            vm(4, 256, 256, dtype=jnp.bfloat16),
-            vm(4, 256, 256, dtype=jnp.bfloat16),
-            vm(16, 16, 128), vm(16, 16, 128), vm(8, 16, 32), vm(8, 32, 512), vm(16, 32, 128), vm(8, 16, 32),
+            vm(256, 1024, dtype=jnp.bfloat16),
+            vm(256, 1024, dtype=jnp.bfloat16),
+            vm(16, 16, 128), vm(16, 16, 128), vm(8, 16, 32), vm(8, 32, 512, dtype=jnp.bfloat16),
+            vm(8, 32, 512, dtype=jnp.bfloat16), vm(16, 32, 128, dtype=jnp.bfloat16),
+            vm(16, 32, 128, dtype=jnp.bfloat16), vm(8, 16, 32),
             vm(32, 1, 128), vm(8, 1, 128), vm(3, 1, 128),
             dma((17,)), dma((13,)), dma((13,)),
         ],

time: 32.9 us -> 32.7 us (level)
  no operation moved by 1% of the time
where the time goes in v6:
time: 32.7 us; the launch traced here: 32.6 us
  Pallas kernels  32.6 us (100%)
    pallas_call x1, Pallas kernels, on_device(): pl.pallas_call(whole_kernel, out_shape=pltpu.VMEM((16, 2048), jnp.float32...  32 us
    pallas_call x1, Pallas kernels, on_device(): pl.pallas_call(store_kernel, out_shape=jax.ShapeDtypeStruct((16, 2048), j...  0.67 us

profile of v6, /device:TPU:1, one launch (start us, length us, event | category | flops | bytes accessed | tf_op | source)
XLA Modules:
  0.0 32.6 jit_solution(13575220626449565147)
XLA Ops:
  0.0 32.0 %whole.1.product = f32[16,2048]{1,0:T(8,128)S(1)} custom-call(s32[16]{0:T(128)} %counts_h.1, s32[1,16]{1,0:T(1,128)} %owner_h.1, s32[1,8]{1,0:T(1,128)} %parent_h.1, s32[16,16]{1,0:T(8,128)} %partners_h.1, s32[8,8]{1,0:T(8,128)} %peers_h.1, s32[8,8]{1,0:T(8,128)} %slots_h.1, s32[16,16]{1,0:T(8,128)} %offsets_h.1, f32[4,8]{1,0:T(4,128)} %bitcast.5, ...), custom_call_target="tpu_custom_call" | custom-call | tf_op jit(solution)/shard_map/whole/pallas_call | solution.py:521
  32.0 0.7 %store.1 = f32[16,2048]{1,0:T(8,128)} custom-call(f32[16,2048]{1,0:T(8,128)S(1)} %whole.1.product), custom_call_target="tpu_custom_call" | custom-call | tf_op jit(solution)/shard_map/store/pallas_call | solution.py:555

commit v7 on v6

--- a/solution.py
+++ b/solution.py
@@ -140,8 +140,8 @@
     def hello(peer):
         pl.semaphore_signal(barrier, inc=1, device_id=peer, device_id_type=MESH)
 
+    others(-1, lambda a, b: hello(plane_peer(a, b)))
     others(NZ, lambda a, b: hello(leaf_peer(a, b)))
-    others(-1, lambda a, b: hello(plane_peer(a, b)))
 
     loads = [
         pltpu.make_async_copy(a, b, s_in.at[i])
@@ -269,16 +269,16 @@
     row = jnp.zeros((1, 128), jnp.float32)
     for c in range(4):
         for i in range(8):
-            row = jnp.where(lane1 == c * 8 + i, mgeo[c, i], row)
+            row = jnp.where(lane1 == i * 4 + c, mgeo[c, i], row)
         for i in range(16):
-            row = jnp.where(lane1 == 32 + c * 16 + i, lgeo[c, i], row)
+            row = jnp.where(lane1 == 32 + i * 4 + c, lgeo[c, i], row)
     geo[...] = row
     geos_v[d] = row
     lgeos_v[1] = row
     row = jnp.zeros((1, 128), jnp.float32)
     for c in range(4):
         for i in range(16):
-            row = jnp.where(lane1 == c * 16 + i, ggeo[c, i], row)
+            row = jnp.where(lane1 == i * 4 + c, ggeo[c, i], row)
     tgeo[...] = row
     tgeos_v[g] = row
 
@@ -378,13 +378,13 @@
         return kappa(squared)
 
     def top_read(s):
-        return lambda c: tgeos[s >> 4, 0, c * 16 + (s & 15)]
+        return lambda c: tgeos[s >> 4, 0, (s & 15) * 4 + c]
 
     def mid_read(i):
-        return lambda c: geos[i >> 3, 0, c * 8 + (i & 7)]
+        return lambda c: geos[i >> 3, 0, (i & 7) * 4 + c]
 
     def leaf_read(w):
-        return lambda c: lgeos[w >> 4, 0, 32 + c * 16 + (w & 15)]
+        return lambda c: lgeos[w >> 4, 0, 32 + (w & 15) * 4 + c]
 
     def make_w(l):
         w_h[l], w_l[l] = split(dot3(leaf_t[l], basis[l], 0, 0))

time: 32.7 us -> 33 us (level)
  no operation moved by 1% of the time
where the time goes in v7:
time: 33 us; the launch traced here: 32.9 us
  Pallas kernels  32.9 us (100%)
    pallas_call x1, Pallas kernels, on_device(): pl.pallas_call(whole_kernel, out_shape=pltpu.VMEM((16, 2048), jnp.float32...  32.2 us
    pallas_call x1, Pallas kernels, on_device(): pl.pallas_call(store_kernel, out_shape=jax.ShapeDtypeStruct((16, 2048), j...  0.67 us

profile of v7, /device:TPU:1, one launch (start us, length us, event | category | flops | bytes accessed | tf_op | source)
XLA Modules:
  0.0 32.9 jit_solution(8457940729095321723)
XLA Ops:
  0.0 32.2 %whole.1.product = f32[16,2048]{1,0:T(8,128)S(1)} custom-call(s32[16]{0:T(128)} %counts_h.1, s32[1,16]{1,0:T(1,128)} %owner_h.1, s32[1,8]{1,0:T(1,128)} %parent_h.1, s32[16,16]{1,0:T(8,128)} %partners_h.1, s32[8,8]{1,0:T(8,128)} %peers_h.1, s32[8,8]{1,0:T(8,128)} %slots_h.1, s32[16,16]{1,0:T(8,128)} %offsets_h.1, f32[4,8]{1,0:T(4,128)} %bitcast.5, ...), custom_call_target="tpu_custom_call" | custom-call | tf_op jit(solution)/shard_map/whole/pallas_call | solution.py:521
  32.2 0.7 %store.1 = f32[16,2048]{1,0:T(8,128)} custom-call(f32[16,2048]{1,0:T(8,128)S(1)} %whole.1.product), custom_call_target="tpu_custom_call" | custom-call | tf_op jit(solution)/shard_map/store/pallas_call | solution.py:555
